TPU v7x, 256 devices: a whole 4x4x8 slice. The times are simulated.
256 devices in a mesh: freq: 32 (over z, x_hi, core), rec: 8 (over y, x_lo).
Axes of the slice: x: 4 (x_hi: 2, x_lo: 2; x = x_hi * 2 + x_lo), y: 4, z: 8, core: 2. Of those that a mesh axis runs over, the one named last changes fastest.
Arguments:
- kernel: bfloat16 [2, 128, 256, 9216], P(None, 'freq', None, 'rec'), may hold values from -0.09375 to 0.09375
- focusing_in: bfloat16 [64, 9216, 1024], P('freq', 'rec'), may hold values from -6 to 6
- onset_src: int32 [64, 256], P('freq'), may hold values from 128 to 895
- onset_rec: int32 [64, 9216], P('freq', 'rec'), may hold values from 128 to 895
Outputs:
- focusing: bfloat16 [64, 9216, 1024], P('freq', 'rec')
- upgoing_field: bfloat16 [64, 256, 1024], P('freq', 'rec')
All inputs are finite; a program needn't handle non-finite values.
Results may differ from a plain program's by a relative error of at most 0.018.
Values may be sent and summed in bfloat16 or wider, within the bound.
No kernel may reach another device: no remote copies, remote signals or barrier semaphores. Data moves between devices by JAX's collectives and lax.ppermute only.
A program may use at most 64 MiB of HBM per device.

v0:
```python
import jax
import jax.numpy as jnp
from jax import lax
from jax.sharding import PartitionSpec as P

LOW = 8
ITERS = 2


def make_tables(count, samples, lowest):
    freqs = (lax.iota(jnp.int32, count) + lowest)[:, None]
    times = lax.iota(jnp.int32, samples)[None, :]
    phase = (freqs * times % samples).astype(jnp.float32) * (2.0 * 3.141592653589793 / samples)
    both = jnp.stack([jnp.cos(phase), -jnp.sin(phase)])
    forward = both.astype(jnp.bfloat16)
    inverse = (forward.astype(jnp.float32) * (2.0 / samples)).astype(jnp.bfloat16)
    return (forward, inverse)


def forward_mdc(block_slice, spread_layout):
    real = jnp.einsum(
        "wch,wah->cwa", block_slice[0], spread_layout[0], preferred_element_type=jnp.float32
    ) - jnp.einsum(
        "wch,wah->cwa", block_slice[1], spread_layout[1], preferred_element_type=jnp.float32
    )
    imag = jnp.einsum(
        "wch,wah->cwa", block_slice[0], spread_layout[1], preferred_element_type=jnp.float32
    ) + jnp.einsum(
        "wch,wah->cwa", block_slice[1], spread_layout[0], preferred_element_type=jnp.float32
    )
    return jnp.stack([real, imag], axis=1)


def adjoint_mdc(block_slice, piece_portion):
    real = jnp.einsum(
        "thl,htv->tvl", block_slice[0], piece_portion[:, 0], preferred_element_type=jnp.float32
    ) + jnp.einsum(
        "thl,htv->tvl", block_slice[1], piece_portion[:, 1], preferred_element_type=jnp.float32
    )
    imag = jnp.einsum(
        "thl,htv->tvl", block_slice[0], piece_portion[:, 1], preferred_element_type=jnp.float32
    ) - jnp.einsum(
        "thl,htv->tvl", block_slice[1], piece_portion[:, 0], preferred_element_type=jnp.float32
    )
    return jnp.stack([real, imag])


def body(kernel, focusing_in, onset_src, onset_rec):
    freq_count = lax.axis_size("freq")
    rec_count = lax.axis_size("rec")
    band = kernel.shape[1] * freq_count
    samples = focusing_in.shape[2]
    sources = kernel.shape[2]
    share = sources // rec_count
    forward, inverse = make_tables(band, samples, LOW)
    times = lax.iota(jnp.int32, samples)
    keep_rec = times[None, None, :] < onset_rec[:, :, None]
    first = lax.axis_index("rec") * share
    focusing = focusing_in
    upgoing_field = None
    for step in range(ITERS):
        spectrum = jnp.einsum(
            "prt,ckt->ckpr", focusing, forward, preferred_element_type=jnp.float32
        ).astype(jnp.bfloat16)
        spread_layout = lax.all_to_all(spectrum, "freq", split_axis=1, concat_axis=2, tiled=True)
        own_onsets = lax.dynamic_slice_in_dim(onset_src, first, share, 1)
        keep_src = times[None, None, :] < own_onsets[:, :, None]
        local = lax.psum_scatter(
            forward_mdc(kernel, spread_layout).astype(jnp.bfloat16),
            "rec",
            scatter_dimension=0,
            tiled=True,
        )
        series = lax.all_to_all(local, "freq", split_axis=3, concat_axis=2, tiled=True)
        signal = jnp.einsum("sckp,ckt->pst", series, inverse, preferred_element_type=jnp.float32)
        upgoing_field = signal.astype(jnp.bfloat16)
        muted = jnp.where(keep_src, signal, 0.0).astype(jnp.bfloat16)
        echo = jnp.einsum(
            "pst,ckt->sckp", muted, forward, preferred_element_type=jnp.float32
        ).astype(jnp.bfloat16)
        returned_output = lax.all_to_all(echo, "freq", split_axis=2, concat_axis=3, tiled=True)
        reflected = adjoint_mdc(kernel, lax.all_gather(returned_output, "rec", axis=0, tiled=True))
        reflected = reflected.astype(jnp.bfloat16)
        arrived = lax.all_to_all(reflected, "freq", split_axis=2, concat_axis=1, tiled=True)
        update = jnp.einsum("ckpr,ckt->prt", arrived, inverse, preferred_element_type=jnp.float32)
        focusing = (focusing_in.astype(jnp.float32) + jnp.where(keep_rec, update, 0.0)).astype(
            jnp.bfloat16
        )
    return (focusing, upgoing_field)


def solution(mesh):
    placed = (
        P(None, "freq", None, "rec"),
        P("freq", "rec", None),
        P("freq", None),
        P("freq", "rec"),
    )
    return jax.shard_map(
        body,
        mesh=mesh,
        in_specs=placed,
        out_specs=(P("freq", "rec", None), P("freq", "rec", None)),
        check_vma=False,
    )
```

profile of v0, /device:TPU:1, one launch (start us, length us, event | category | flops | bytes accessed | tf_op | source)
XLA Modules:
  0.0 511.5 jit_solution(12522489238005167587)
XLA Ops:
  7.2 2.4 cosine_convert_fusion
  9.7 3.8 fusion.6
  13.5 1.2 copy.54
  14.7 45.1 %all_to_all.138 = bf16[2,128,2,1152]{3,2,0,1:T(2,128)(2,1)S(1)} all-to-all(bf16[2,128,2,1152]{3,2,0,1:T(2,128)(2,1)S(1)} %copy.54), channel_id=1, replica_groups=mesh['freq'=32,'rec'=8] {'freq'}, dimensions={1} | all-to-all | bytes 2359296 | tf_op jit(solution)/shard_map/all_to_all | solution.py:65
  59.8 0.8 copy.105
  60.7 0.8 fusion.154
  61.5 0.2 squeeze.22
  61.7 0.2 squeeze.20
  61.9 2.6 fusion.30
  64.6 2.5 fusion.28
  67.1 2.5 fusion.78
  69.6 0.8 fusion.81
  70.5 1.1 copy.56
  71.6 0.6 dynamic-slice
  72.9 70.0 %all-reduce.5.cloned.1.call-done = bf16[256,2,4,64]{3,2,1,0:T(4,128)(2,1)} async-done(((bf16[256,2,4,64]{3,2,1,0:T(4,128)(2,1)}), bf16[256,2,4,64]{3,2,1,0:T(4,128)(2,1)}) %all-reduce.5.cloned.1.call-update) | async-done | bytes 262160
  142.9 0.9 constant_dynamic-slice_fusion.1
  143.7 0.1 copy.57
  143.9 0.8 reshape.130
  144.6 15.2 %all-to-all-start.1 = ((bf16[32,2,256]{2,1,0:T(2,128)(2,1)}), bf16[32,2,256]{2,1,0:T(2,128)(2,1)S(1)}, u32[]{:S(2)}, u32[]{:S(2)}) async-start(bf16[32,2,256]{2,1,0:T(2,128)(2,1)} %reshape.130), calls=%async_computation.1 | async-start | bytes 65536 | tf_op jit(solution)/shard_map/all_to_all | solution.py:74
  160.0 9.5 %all-to-all-done.1 = bf16[32,2,256]{2,1,0:T(2,128)(2,1)S(1)} async-done(((bf16[32,2,256]{2,1,0:T(2,128)(2,1)}), bf16[32,2,256]{2,1,0:T(2,128)(2,1)S(1)}, u32[]{:S(2)}, u32[]{:S(2)}) %all-to-all-start.1) | async-done | bytes 32800 | tf_op jit(solution)/shard_map/all_to_all | solution.py:74
  169.7 0.4 fusion.90
  170.4 12.8 %all_to_all.139 = bf16[32,2,256]{2,1,0:T(2,128)(2,1)S(1)} all-to-all(bf16[32,2,256]{2,1,0:T(2,128)(2,1)S(1)} %reshape.132), channel_id=1, replica_groups=mesh['freq'=32,'rec'=8] {'freq'}, dimensions={0} | all-to-all | bytes 65536 | tf_op jit(solution)/shard_map/all_to_all | solution.py:81
  183.6 24.7 %all_gather.6 = bf16[256,2,4,64]{3,2,1,0:T(4,128)(2,1)S(1)} all-gather(bf16[32,2,4,64]{3,2,1,0:T(4,128)(2,1)S(1)} %copy.63), channel_id=1, replica_groups=mesh['freq'=32,'rec'=8] {'rec'}, dimensions={0}, use_global_device_ids=true | all-gather | bytes 294912 | tf_op jit(solution)/shard_map/all_gather | solution.py:82
  208.3 0.2 fusion.156
  208.5 0.2 copy.93
  208.7 0.2 copy.94
  208.8 2.3 fusion.40
  211.2 2.2 fusion.42
  213.4 2.1 fusion.18
  215.6 0.5 fusion.19
  216.2 0.9 copy.66
  217.1 41.4 %all_to_all.140 = bf16[2,4,64,1152]{3,1,0,2:T(4,128)(2,1)S(1)} all-to-all(bf16[2,4,64,1152]{3,1,0,2:T(4,128)(2,1)S(1)} %copy.66), channel_id=1, replica_groups=mesh['freq'=32,'rec'=8] {'freq'}, dimensions={2} | all-to-all | bytes 2359296 | tf_op jit(solution)/shard_map/all_to_all | solution.py:84
  258.5 0.9 copy.67
  259.5 5.4 %fusion.9 = bf16[2,128,2,1152]{3,1,2,0:T(8,128)(2,1)S(1)} fusion(bf16[2,1152,1024]{2,1,0:T(8,128)(2,1)} %param.5, s32[2,1152]{1,0:T(2,128)S(1)} %copy-done.1, bf16[2,128,2,1152]{3,2,1,0:T(2,128)(2,1)S(1)} %bitcast.248, bf16[1,128,1024]{2,1,0:T(8,128)(2,1)S(1)} %get-tuple-element.11, bf16[1,128,1024]{2,1,0:T(8,128)(2,1)S(1)} %get-tuple-element.10), kind=kOutput, calls=%fused_computation.12 | convolution fusion | flops 2430402560 | bytes 7611392 | tf_op jit(solution)/shard_map/prt,ckt->ckpr/dot_general | solution.py:62
  264.9 1.2 copy.69
  266.1 36.5 %all_to_all.141 = bf16[2,128,2,1152]{3,2,0,1:T(2,128)(2,1)S(1)} all-to-all(bf16[2,128,2,1152]{3,2,0,1:T(2,128)(2,1)S(1)} %copy.69), channel_id=1, replica_groups=mesh['freq'=32,'rec'=8] {'freq'}, dimensions={1} | all-to-all | bytes 2359296 | tf_op jit(solution)/shard_map/all_to_all | solution.py:65
  302.6 0.8 copy.104
  303.4 0.8 fusion.153
  304.2 0.2 squeeze.27
  304.5 2.5 fusion.24
  307.0 0.2 squeeze.26
  307.2 2.5 fusion.22
  309.7 2.5 fusion.84
  312.3 2.5 fusion.87
  314.8 1.1 copy.71
  315.9 69.1 %all-reduce.7.cloned.1.call-done = bf16[256,2,4,64]{3,2,1,0:T(4,128)(2,1)} async-done(((bf16[256,2,4,64]{3,2,1,0:T(4,128)(2,1)}), bf16[256,2,4,64]{3,2,1,0:T(4,128)(2,1)}) %all-reduce.7.cloned.1.call-update) | async-done | bytes 262160
  385.0 0.9 constant_dynamic-slice_fusion
  385.9 0.1 copy.72
  386.2 24.7 %all_to_all.142 = bf16[32,2,256]{2,1,0:T(2,128)(2,1)S(1)} all-to-all(bf16[32,2,256]{2,1,0:T(2,128)(2,1)S(1)} %reshape.134), channel_id=1, replica_groups=mesh['freq'=32,'rec'=8] {'freq'}, dimensions={0} | all-to-all | bytes 65536 | tf_op jit(solution)/shard_map/all_to_all | solution.py:74
  411.0 0.2 convolution_bitcast_fusion
  411.3 0.3 fusion.91
  411.9 12.8 %all_to_all.143 = bf16[32,2,256]{2,1,0:T(2,128)(2,1)S(1)} all-to-all(bf16[32,2,256]{2,1,0:T(2,128)(2,1)S(1)} %reshape.136), channel_id=1, replica_groups=mesh['freq'=32,'rec'=8] {'freq'}, dimensions={0} | all-to-all | bytes 65536 | tf_op jit(solution)/shard_map/all_to_all | solution.py:81
  425.1 24.5 %all_gather.7 = bf16[256,2,4,64]{3,2,1,0:T(4,128)(2,1)S(1)} all-gather(bf16[32,2,4,64]{3,2,1,0:T(4,128)(2,1)S(1)} %copy.78), channel_id=1, replica_groups=mesh['freq'=32,'rec'=8] {'rec'}, dimensions={0}, use_global_device_ids=true | all-gather | bytes 294912 | tf_op jit(solution)/shard_map/all_gather | solution.py:82
  449.6 0.2 fusion.155
  449.8 0.2 copy.95
  449.9 0.2 copy.96
  450.1 2.3 fusion.32
  452.4 2.2 fusion.34
  454.7 2.3 fusion.16
  457.0 0.5 fusion.17
  457.6 0.9 copy.81
  458.6 41.4 %all_to_all.144 = bf16[2,4,64,1152]{3,1,0,2:T(4,128)(2,1)S(1)} all-to-all(bf16[2,4,64,1152]{3,1,0,2:T(4,128)(2,1)S(1)} %copy.81), channel_id=1, replica_groups=mesh['freq'=32,'rec'=8] {'freq'}, dimensions={2} | all-to-all | bytes 2359296 | tf_op jit(solution)/shard_map/all_to_all | solution.py:84
  500.0 0.9 copy.82
  500.9 3.8 fusion.1
  (55 shorter events, 2.4 us)
Async XLA Ops:
  7.2 152.8 %copy-start = (s32[2,256]{1,0:T(2,128)S(1)}, s32[2,256]{1,0:T(2,128)}, u32[]{:S(2)}) copy-start(s32[2,256]{1,0:T(2,128)} %param.6) | copy-start | bytes 6148
  7.2 135.7 %all-reduce.5.cloned.1.call-start = ((), (), s32[]{:S(2)}) async-start(), calls=%async_computation.8 | async-start | bytes 1048576
  60.6 9.0 %slice-start = ((s8[4718592]{0:T(1024)(128)(4,1)}), s8[524288]{0:T(1024)(128)(4,1)S(1)}, s32[]{:S(2)}) async-start(s8[4718592]{0:T(1024)(128)(4,1)} %bitcast.235), calls=%async_computation.10 | async-start | bytes 1048576
  61.9 7.7 %slice-start.1 = ((s8[4718592]{0:T(1024)(128)(4,1)}), s8[4194304]{0:T(1024)(128)(4,1)S(1)}, s32[]{:S(2)}) async-start(s8[4718592]{0:T(1024)(128)(4,1)} %bitcast.235), calls=%async_computation.11 | async-start | bytes 8388608
  69.6 2.0 copy-start.3
  144.6 24.9 %all-to-all-start.1 = ((bf16[32,2,256]{2,1,0:T(2,128)(2,1)}), bf16[32,2,256]{2,1,0:T(2,128)(2,1)S(1)}, u32[]{:S(2)}, u32[]{:S(2)}) async-start(bf16[32,2,256]{2,1,0:T(2,128)(2,1)} %reshape.130), calls=%async_computation.1 | async-start | bytes 65536 | tf_op jit(solution)/shard_map/all_to_all | solution.py:74
  159.9 225.2 %all-reduce.7.cloned.1.call-start = ((), (), s32[]{:S(2)}) async-start(), calls=%async_computation.9 | async-start | bytes 1048576
  208.8 6.7 %slice-start.2 = ((s8[4718592]{0:T(1024)(128)(4,1)}), s8[4194304]{0:T(1024)(128)(4,1)S(1)}, s32[]{:S(2)}) async-start(s8[4718592]{0:T(1024)(128)(4,1)} %bitcast.237), calls=%async_computation.12 | async-start | bytes 8388608
  211.2 4.4 slice-start.3
  217.1 42.4 %copy-start.1 = (s32[2,1152]{1,0:T(2,128)S(1)}, s32[2,1152]{1,0:T(2,128)}, u32[]{:S(2)}) copy-start(s32[2,1152]{1,0:T(2,128)} %param.7) | copy-start | bytes 27652
  411.3 38.8 %copy-start.2 = (bf16[2,32,1024]{2,1,0:T(8,128)(2,1)}, bf16[2,32,1024]{2,1,0:T(8,128)(2,1)S(1)}, u32[]{:S(2)}) copy-start(bf16[2,32,1024]{2,1,0:T(8,128)(2,1)S(1)} %convolution_bitcast_fusion) | copy-start | bytes 393220
  450.1 6.9 %slice-start.4 = ((s8[4718592]{0:T(1024)(128)(4,1)}), s8[4194304]{0:T(1024)(128)(4,1)S(1)}, s32[]{:S(2)}) async-start(s8[4718592]{0:T(1024)(128)(4,1)} %bitcast.239), calls=%async_computation.14 | async-start | bytes 8388608
  452.4 4.6 slice-start.5
  454.7 46.2 %slice-start.6 = ((s8[4718592]{0:T(1024)(128)(4,1)}), s8[4194304]{0:T(1024)(128)(4,1)S(1)}, s32[]{:S(2)}) async-start(s8[4718592]{0:T(1024)(128)(4,1)} %bitcast.263), calls=%async_computation.16 | async-start | bytes 8388608
  457.5 43.4 %slice-start.7 = ((s8[4718592]{0:T(1024)(128)(4,1)}), s8[524288]{0:T(1024)(128)(4,1)S(1)}, s32[]{:S(2)}) async-start(s8[4718592]{0:T(1024)(128)(4,1)} %bitcast.263), calls=%async_computation.17 | async-start | bytes 1048576
Sparse Core Ops, SparseCore 0:
  71.7 71.0 all-reduce.4
  316.0 68.9 all-reduce.6
where the time goes:
time: 512 us
  blocking collectives  264 us (52%)
  waiting for transfers between devices  149 us (29%)
  matrix products  46.9 us (9%)
  local copies, waits for them, and re-layouts  18.7 us (4%)
  between operations  15.4 us (3%)
  starting transfers between devices  15.3 us (3%)
    unnamed x4, waiting for transfers between devices  139 us
    all_to_all x2, blocking collectives, body(): lax.all_to_all(reflected, 'freq', split_axis=2, concat_axis=1, tiled=True)  82.8 us
    all_to_all x2, blocking collectives, body(): lax.all_to_all(spectrum, 'freq', split_axis=1, concat_axis=2, tiled=True)  81.6 us
    all_gather x2, blocking collectives, body(): lax.all_gather(returned_output, 'rec', axis=0, tiled=True)  49.2 us
    all_to_all x2, blocking collectives, body(): lax.all_to_all(echo, 'freq', split_axis=2, concat_axis=3, tiled=True)  25.5 us
    all_to_all x1, blocking collectives, body(): lax.all_to_all(local, 'freq', split_axis=3, concat_axis=2, tiled=True)  24.7 us
    all_to_all x1, starting transfers between devices, body(): lax.all_to_all(local, 'freq', split_axis=3, concat_axis=2, tiled=True)  15.2 us
  transfers between devices with their start and end apart: 3, of which 3 were waited for; matrix products, arithmetic and copies ran while one was open for 0% of the time, Pallas kernels for 0%

commit v1 on v0

v1 whole, which is shorter than its diff:
```python
import functools

import jax
import jax.numpy as jnp
import numpy as np
from jax import lax
from jax.experimental import pallas as pl
from jax.experimental.pallas import tpu as pltpu
from jax.sharding import PartitionSpec as P

LOW = 8
ITERS = 2
SPLIT = False
F32 = jnp.float32
BF16 = jnp.bfloat16
NN = (((1,), (0,)), ((), ()))
NT = (((1,), (1,)), ((), ()))
TN = (((0,), (0,)), ((), ()))


def dot(a, b, dims=NN):
    return lax.dot_general(a, b, dims, preferred_element_type=F32)


def make_table(freq, own, samples):
    k = np.arange(freq * own)[:, None] + LOW
    t = np.arange(samples)[None, :]
    phase = ((k * t) % samples).astype(np.float32) * np.float32(2.0 * 3.141592653589793 / samples)
    both = np.stack([np.cos(phase), -np.sin(phase)]).astype(np.float32)
    rows = both.reshape(2, freq, own, samples).transpose(1, 0, 2, 3)
    return jnp.asarray(rows.reshape(freq * 2 * own, samples), BF16)


def make_order(freq, points, own):
    n = freq * points * 2 * own
    rows = np.arange(n).reshape(freq, points, 2, own).transpose(3, 2, 0, 1).reshape(n)
    return jnp.asarray(np.eye(n, dtype=np.float32)[rows], BF16)


def make_pairs(freq, points):
    n = freq * points * 2
    rows = np.arange(n).reshape(2, freq, points).transpose(1, 2, 0).reshape(n)
    return jnp.asarray(np.eye(n, dtype=np.float32)[rows], BF16)


def whole(shape):
    return pl.BlockSpec(shape, lambda *_: (0,) * len(shape))


def cost(flops, bytes_accessed):
    return pl.CostEstimate(flops=int(flops), transcendentals=0, bytes_accessed=int(bytes_accessed))


def spectrum_rows(fs, table, freq):
    parts = [dot(table, f, NT) for f in fs]
    parts = [s.reshape(freq, s.shape[0] // freq, s.shape[1]) for s in parts]
    return jnp.concatenate(parts, axis=1).astype(BF16)


def spectrum_kernel(f_ref, table_ref, out_ref):
    fs = [f_ref[p] for p in range(f_ref.shape[0])]
    out_ref[...] = spectrum_rows(fs, table_ref[...], out_ref.shape[0])


def spectrum(f, table, freq, block=384):
    points, receivers, samples = f.shape
    rows = points * table.shape[0] // freq
    return pl.pallas_call(
        spectrum_kernel,
        grid=(receivers // block,),
        in_specs=[pl.BlockSpec((points, block, samples), lambda i: (0, i, 0)), whole(table.shape)],
        out_specs=pl.BlockSpec((freq, rows, block), lambda i: (0, 0, i)),
        out_shape=jax.ShapeDtypeStruct((freq, rows, receivers), BF16),
        cost_estimate=cost(2 * f.size * table.shape[0], 2 * (f.size + freq * rows * receivers)),
        name="spectrum",
    )(f, table)


def product_kernel(k_ref, x_ref, order_ref, pairs_ref, out_ref, w, g):
    step = pl.program_id(0)
    own, rows, receivers = w.shape
    half = rows // 2
    blocks, _, width = out_ref.shape
    share = width // own

    @pl.when(step == 0)
    def _():
        x = x_ref[...].reshape(own * rows, receivers)
        w[...] = dot(order_ref[...], x).astype(BF16).reshape(w.shape)

    w0 = w[step]
    w1 = jnp.concatenate([-w0[half:], w0[:half]], axis=0)
    total = dot(w0, k_ref[0, 0], NT) + dot(w1, k_ref[1, 0], NT)
    g[step] = dot(pairs_ref[...], total.astype(BF16))

    @pl.when(step == own - 1)
    def _():
        for j in range(blocks):
            parts = [g[kk, :, j * share : (j + 1) * share] for kk in range(own)]
            out_ref[j] = jnp.concatenate(parts, axis=1).astype(BF16)


def product(kernel, x, order, pairs, blocks):
    _, own, sources, receivers = kernel.shape
    rows = order.shape[0] // own
    width = own * sources // blocks
    return pl.pallas_call(
        product_kernel,
        grid=(own,),
        in_specs=[
            pl.BlockSpec((2, 1, sources, receivers), lambda i: (0, i, 0, 0)),
            whole(x.shape),
            whole(order.shape),
            whole(pairs.shape),
        ],
        out_specs=whole((blocks, rows, width)),
        out_shape=jax.ShapeDtypeStruct((blocks, rows, width), BF16),
        scratch_shapes=[
            pltpu.VMEM((own, rows, receivers), BF16),
            pltpu.VMEM((own, rows, sources), F32),
        ],
        cost_estimate=cost(2 * kernel.size * rows, 2 * (kernel.size + x.size)),
        name="product",
    )(kernel, x, order, pairs)


def source_kernel(points, keep_field, v_ref, onset_ref, table_ref, h_ref, *field_ref):
    rows, samples = table_ref.shape
    lines, width = h_ref.shape
    share = onset_ref.shape[1]
    own = width // share
    table = table_ref[...]
    v = v_ref[...].astype(F32)
    if v.ndim == 3:
        v = jnp.sum(v, axis=0)
    v = v.astype(BF16)
    row = lax.broadcasted_iota(jnp.int32, (rows, lines), 0)
    line = lax.broadcasted_iota(jnp.int32, (rows, lines), 1)
    device, part, mine = row // (2 * own), row // own % 2, row % own
    h = [jnp.zeros((lines, share), F32) for _ in range(own)]
    for p in range(points):
        at = (device * points + p) * 2 + part
        picks = [jnp.where((line == at) & (mine == kk), 1.0, 0.0).astype(BF16) for kk in range(own)]
        full = jnp.zeros((rows, share), F32)
        for kk in range(own):
            full = full + dot(picks[kk], v[:, kk * share : (kk + 1) * share])
        g = dot(full.astype(BF16), table, TN) * (2.0 / samples)
        if keep_field:
            field_ref[0][p] = g.astype(BF16)
        times = lax.broadcasted_iota(jnp.int32, g.shape, 1)
        muted = jnp.where(times < onset_ref[p], g, 0.0).astype(BF16)
        back = dot(table, muted, NT).astype(BF16)
        for kk in range(own):
            h[kk] = h[kk] + dot(picks[kk], back, TN)
    h_ref[...] = jnp.concatenate(h, axis=1).astype(BF16)


def source_step(v, onset, table, keep_field):
    samples = table.shape[1]
    points, share, _ = onset.shape
    out_shape = [jax.ShapeDtypeStruct(v.shape[-2:], BF16)]
    if keep_field:
        out_shape.append(jax.ShapeDtypeStruct((points, share, samples), BF16))
    return pl.pallas_call(
        functools.partial(source_kernel, points, keep_field),
        out_shape=out_shape,
        cost_estimate=cost(4 * v.size * samples, 2 * table.size),
        name="source",
    )(v, onset, table)


def adjoint_kernel(k_ref, u_ref, pairs_ref, order_ref, out_ref, l, o):
    step = pl.program_id(0)
    own, rows, _ = l.shape
    half = rows // 2
    blocks, _, width = u_ref.shape
    share = width // own

    @pl.when(step == 0)
    def _():
        for kk in range(own):
            parts = [u_ref[j, :, kk * share : (kk + 1) * share] for j in range(blocks)]
            full = jnp.concatenate(parts, axis=1)
            l[kk] = dot(pairs_ref[...], full, TN).astype(BF16)

    l0 = l[step]
    l1 = jnp.concatenate([l0[half:], -l0[:half]], axis=0)
    o[step] = (dot(l0, k_ref[0, 0]) + dot(l1, k_ref[1, 0])).astype(BF16)

    @pl.when(step == own - 1)
    def _():
        flat = o[...].reshape(own * rows, o.shape[2])
        out_ref[...] = dot(order_ref[...], flat, TN).astype(BF16).reshape(out_ref.shape)


def adjoint(kernel, u, pairs, order, freq):
    _, own, sources, receivers = kernel.shape
    rows = u.shape[1]
    out = (freq, own * rows // freq, receivers)
    return pl.pallas_call(
        adjoint_kernel,
        grid=(own,),
        in_specs=[
            pl.BlockSpec((2, 1, sources, receivers), lambda i: (0, i, 0, 0)),
            whole(u.shape),
            whole(pairs.shape),
            whole(order.shape),
        ],
        out_specs=whole(out),
        out_shape=jax.ShapeDtypeStruct(out, BF16),
        scratch_shapes=[
            pltpu.VMEM((own, rows, sources), BF16),
            pltpu.VMEM((own, rows, receivers), BF16),
        ],
        cost_estimate=cost(2 * kernel.size * rows, 2 * (kernel.size + own * rows * receivers)),
        name="adjoint",
    )(kernel, u, pairs, order)


def update_kernel(last, q_ref, f_ref, onset_ref, table_ref, out_ref):
    table = table_ref[...]
    freq, rows, block = q_ref.shape
    points, _, samples = f_ref.shape
    each = rows // points
    spectra = q_ref[...].astype(F32)
    times = lax.broadcasted_iota(jnp.int32, (block, samples), 1)
    fs = []
    for p in range(points):
        mine = spectra[:, p * each : (p + 1) * each].reshape(freq * each, block).astype(BF16)
        q = dot(mine, table, TN) * (2.0 / samples)
        f = f_ref[p].astype(F32) + jnp.where(times < onset_ref[p], q, 0.0)
        fs.append(f.astype(BF16))
    if last:
        for p in range(points):
            out_ref[p] = fs[p]
    else:
        out_ref[...] = spectrum_rows(fs, table, freq)


def update(q, f, onset, table, last, block=384):
    points, receivers, samples = f.shape
    freq, rows, _ = q.shape
    spec_block = pl.BlockSpec((freq, rows, block), lambda i: (0, 0, i))
    trace_block = pl.BlockSpec((points, block, samples), lambda i: (0, i, 0))
    return pl.pallas_call(
        functools.partial(update_kernel, last),
        grid=(receivers // block,),
        in_specs=[spec_block, trace_block, pl.BlockSpec((points, block, 1), lambda i: (0, i, 0)), whole(table.shape)],
        out_specs=trace_block if last else spec_block,
        out_shape=jax.ShapeDtypeStruct(f.shape if last else q.shape, BF16),
        cost_estimate=cost(4 * f.size * table.shape[0], 2 * (2 * f.size + q.size)),
        name="update",
    )(q, f, onset, table)


def exchange(x, axis):
    return lax.all_to_all(x, axis, split_axis=0, concat_axis=0, tiled=True)


def body(kernel, focusing_in, onset_src, onset_rec):
    freq = lax.axis_size("freq")
    rec = lax.axis_size("rec")
    _, own, sources, receivers = kernel.shape
    points, _, samples = focusing_in.shape
    share = sources // rec
    lines, width = freq * points * 2, own * share
    table = make_table(freq, own, samples)
    order = make_order(freq, points, own)
    pairs = make_pairs(freq, points)
    first = lax.axis_index("rec") * share
    src_onsets = lax.dynamic_slice_in_dim(onset_src, first, share, 1)[:, :, None]
    rec_onsets = onset_rec[:, :, None]
    spec = spectrum(focusing_in, table, freq)
    field = None
    for step in range(ITERS):
        last = step == ITERS - 1
        part = product(kernel, exchange(spec, "freq"), order, pairs, rec)
        if SPLIT:
            v = jnp.sum(exchange(part, "rec").astype(F32), axis=0).astype(BF16)
            v = exchange(v.reshape(freq, points * 2, width), "freq").reshape(lines, width)
        else:
            v = exchange(part.reshape(rec * freq, points * 2, width), ("rec", "freq"))
            v = v.reshape(rec, lines, width)
        h, *kept = source_step(v, src_onsets, table, last)
        if last:
            field = kept[0]
        if SPLIT:
            u = exchange(h.reshape(freq, points * 2, width), "freq").reshape(1, lines, width)
            u = exchange(jnp.broadcast_to(u, (rec, lines, width)), "rec")
        else:
            u = jnp.broadcast_to(h.reshape(1, freq, points * 2, width), (rec, freq, points * 2, width))
            u = exchange(u.reshape(rec * freq, points * 2, width), ("rec", "freq")).reshape(rec, lines, width)
        q = exchange(adjoint(kernel, u, pairs, order, freq), "freq")
        spec = update(q, focusing_in, rec_onsets, table, last)
    return spec, field


def solution(mesh):
    placed = (
        P(None, "freq", None, "rec"),
        P("freq", "rec", None),
        P("freq", None),
        P("freq", "rec"),
    )
    return jax.shard_map(
        body,
        mesh=mesh,
        in_specs=placed,
        out_specs=(P("freq", "rec", None), P("freq", "rec", None)),
        check_vma=False,
    )
```

time: 512 us -> 303 us (0.59)
  waiting for transfers between devices: 149 us -> 44.1 us
  blocking collectives: 264 us -> 187 us
  Pallas kernels: 0 us -> 52.6 us
  matrix products: 46.9 us -> 0 us
  between operations: 15.4 us -> 0.69 us
  local copies, waits for them, and re-layouts: 18.7 us -> 5.63 us
    unnamed x4 -> x0, waiting for transfers between devices: 139 us -> none
    pallas_call x0 -> x9, Pallas kernels: none -> 52.6 us  [the longest x2 14.3 us: update(): pl.pallas_call(functools.partial(update_kernel, last), grid=(receivers //...]
    all_gather x2 -> x0, blocking collectives: 49.2 us -> none  [body(): lax.all_gather(returned_output, 'rec', axis=0, tiled=True)]
    dot_general x22 -> x0, matrix products: 46.9 us -> none  [the longest x2 9.2 us: body(): jnp.einsum('prt,ckt->ckpr', focusing, forward, preferred_element_type=jnp...]
    all_to_all x1 -> x2, waiting for transfers between devices: 9.49 us -> 44.1 us  [exchange(): return lax.all_to_all(x, axis, split_axis=0, concat_axis=0, tiled=True)]
    all_to_all x7 -> x6, blocking collectives: 215 us -> 187 us  [exchange(): return lax.all_to_all(x, axis, split_axis=0, concat_axis=0, tiled=True)]
    all_to_all x1 -> x2, starting transfers between devices: 15.2 us -> 11.2 us  [exchange(): return lax.all_to_all(x, axis, split_axis=0, concat_axis=0, tiled=True)]
  transfers between devices with their start and end apart: 3 -> 2, of which waited for: 3 -> 2; matrix products, arithmetic and copies ran while one was open for 0% -> 1% of each run, Pallas kernels for 0% -> 0%
where the time goes in v1:
time: 303 us; the launch traced here: 302 us
  blocking collectives  187 us (62%)
  Pallas kernels  52.6 us (17%)
  waiting for transfers between devices  44.1 us (15%)
  starting transfers between devices  11.2 us (4%)
  local copies, waits for them, and re-layouts  5.63 us (2%)
    all_to_all x6, blocking collectives, exchange(): return lax.all_to_all(x, axis, split_axis=0, concat_axis=0, tiled=True)  187 us
    all_to_all x2, waiting for transfers between devices, exchange(): return lax.all_to_all(x, axis, split_axis=0, concat_axis=0, tiled=True)  44.1 us
    pallas_call x2, Pallas kernels, update(): pl.pallas_call(functools.partial(update_kernel, last), grid=(receivers //...  14.3 us
    pallas_call x2, Pallas kernels, product(): pl.pallas_call(product_kernel, grid=(own,), in_specs=[pl.BlockSpec((2, 1,...  13.8 us
    pallas_call x2, Pallas kernels, adjoint(): pl.pallas_call(adjoint_kernel, grid=(own,), in_specs=[pl.BlockSpec((2, 1,...  12.7 us
    all_to_all x2, starting transfers between devices, exchange(): return lax.all_to_all(x, axis, split_axis=0, concat_axis=0, tiled=True)  11.2 us
    pallas_call x2, Pallas kernels, source_step(): pl.pallas_call(functools.partial(source_kernel, points, keep_field), out_...  6.52 us
  transfers between devices with their start and end apart: 2, of which 2 were waited for; matrix products, arithmetic and copies ran while one was open for 1% of the time, Pallas kernels for 0%

profile of v1, /device:TPU:1, one launch (start us, length us, event | category | flops | bytes accessed | tf_op | source)
XLA Modules:
  0.0 301.5 jit_solution(14589894647981933096)
XLA Ops:
  0.6 0.0 copy-start
  0.6 5.3 %spectrum.1 = bf16[32,16,1152]{2,1,0:T(8,128)(2,1)} custom-call(bf16[2,1152,1024]{2,1,0:T(8,128)(2,1)} %f_ref.5, bf16[256,1024]{1,0:T(8,128)(2,1)} %constant.16.clone.table_ref), custom_call_target="tpu_custom_call" | custom-call | flops 1207959552 | bytes 5898240 | tf_op jit(solution)/shard_map/spectrum/pallas_call | solution.py:68
  5.9 45.4 %all_to_all.40.x_ref = bf16[32,16,1152]{2,1,0:T(8,128)(2,1)} all-to-all(bf16[32,16,1152]{2,1,0:T(8,128)(2,1)} %spectrum.1), channel_id=1, replica_groups=mesh['freq'=32,'rec'=8] {'freq'}, dimensions={0} | all-to-all | bytes 2359296 | tf_op jit(solution)/shard_map/all_to_all | solution.py:257
  51.4 6.9 %product.2 = bf16[8,128,128]{2,1,0:T(8,128)(2,1)} custom-call(bf16[2,4,256,1152]{3,2,1,0:T(8,128)(2,1)} %k_ref.7, bf16[32,16,1152]{2,1,0:T(8,128)(2,1)} %all_to_all.40.x_ref, bf16[512,512]{1,0:T(8,128)(2,1)} %constant.17.clone.order_ref, bf16[128,128]{1,0:T(8,128)(2,1)} %constant.18.clone.pairs_ref), custom_call_target="tpu_custom_call" | custom-call | flops 603979776 | bytes 5898240 | tf_op jit(solution)/shard_map/product/pallas_call | solution.py:107
  58.3 7.0 %all-to-all-start.1 = ((bf16[256,4,128]{2,1,0:T(4,128)(2,1)}), bf16[256,4,128]{2,1,0:T(4,128)(2,1)S(1)}, u32[]{:S(2)}, u32[]{:S(2)}) async-start(bf16[256,4,128]{2,1,0:T(4,128)(2,1)} %bitcast.13), calls=%async_computation.1 | async-start | bytes 524288 | tf_op jit(solution)/shard_map/all_to_all | solution.py:257
  65.3 0.0 copy-done
  65.3 0.1 dynamic-slice_bitcast_fusion
  65.4 0.7 copy.11.onset_ref
  66.1 14.7 %all-to-all-done.1 = bf16[256,4,128]{2,1,0:T(4,128)(2,1)S(1)} async-done(((bf16[256,4,128]{2,1,0:T(4,128)(2,1)}), bf16[256,4,128]{2,1,0:T(4,128)(2,1)S(1)}, u32[]{:S(2)}, u32[]{:S(2)}) %all-to-all-start.1) | async-done | bytes 262176 | tf_op jit(solution)/shard_map/all_to_all | solution.py:257
  80.8 0.0 copy-start.2
  80.8 0.7 copy-done.2
  81.5 3.3 %source.2 = bf16[128,128]{1,0:T(8,128)(2,1)} custom-call(bf16[8,128,128]{2,1,0:T(8,128)(2,1)} %bitcast.19, s32[2,32,1]{2,1,0:T(8,128)} %copy.11.onset_ref, bf16[256,1024]{1,0:T(8,128)(2,1)} %constant.16.clone.table_ref), custom_call_target="tpu_custom_call" | custom-call | flops 536870912 | bytes 524288 | tf_op jit(solution)/shard_map/source/pallas_call | solution.py:164
  84.8 0.8 broadcast_in_dim.22
  85.6 21.3 %all_to_all.41 = bf16[256,4,128]{2,1,0:T(4,128)(2,1)} all-to-all(bf16[256,4,128]{2,1,0:T(4,128)(2,1)S(1)} %bitcast.17), channel_id=1, replica_groups=mesh['freq'=32,'rec'=8] {'rec','freq'}, dimensions={0} | all-to-all | bytes 524288 | tf_op jit(solution)/shard_map/all_to_all | solution.py:257
  107.0 6.3 %adjoint.2 = bf16[32,16,1152]{2,1,0:T(8,128)(2,1)} custom-call(bf16[2,4,256,1152]{3,2,1,0:T(8,128)(2,1)} %k_ref.7, bf16[8,128,128]{2,1,0:T(8,128)(2,1)} %bitcast.15, bf16[128,128]{1,0:T(8,128)(2,1)} %constant.18.clone.pairs_ref, bf16[512,512]{1,0:T(8,128)(2,1)} %constant.17.clone.order_ref), custom_call_target="tpu_custom_call" | custom-call | flops 603979776 | bytes 5898240 | tf_op jit(solution)/shard_map/adjoint/pallas_call | solution.py:200
  113.3 0.0 copy-start.3
  113.3 4.2 %all-to-all-start.3 = ((bf16[32,16,1152]{2,1,0:T(8,128)(2,1)}), bf16[32,16,1152]{2,1,0:T(8,128)(2,1)S(1)}, u32[]{:S(2)}, u32[]{:S(2)}) async-start(bf16[32,16,1152]{2,1,0:T(8,128)(2,1)} %adjoint.2), calls=%async_computation.3 | async-start | bytes 2359296 | tf_op jit(solution)/shard_map/all_to_all | solution.py:257
  117.5 0.0 copy-done.3
  117.5 1.4 copy.12.onset_ref
  118.9 29.4 %all-to-all-done.3.q_ref = bf16[32,16,1152]{2,1,0:T(8,128)(2,1)S(1)} async-done(((bf16[32,16,1152]{2,1,0:T(8,128)(2,1)}), bf16[32,16,1152]{2,1,0:T(8,128)(2,1)S(1)}, u32[]{:S(2)}, u32[]{:S(2)}) %all-to-all-start.3) | async-done | bytes 1179680 | tf_op jit(solution)/shard_map/all_to_all | solution.py:257
  148.3 0.0 copy-start.1
  148.3 1.0 copy-done.1
  149.3 6.9 %update.2 = bf16[32,16,1152]{2,1,0:T(8,128)(2,1)} custom-call(bf16[32,16,1152]{2,1,0:T(8,128)(2,1)} %copy-done.1, bf16[2,1152,1024]{2,1,0:T(8,128)(2,1)} %f_ref.5, s32[2,1152,1]{2,1,0:T(8,128)} %copy.12.onset_ref, bf16[256,1024]{1,0:T(8,128)(2,1)} %constant.16.clone.table_ref), custom_call_target="tpu_custom_call" | custom-call | flops 2415919104 | bytes 10616832 | tf_op jit(solution)/shard_map/update/pallas_call | solution.py:245
  156.3 38.7 %all_to_all.42.x_ref = bf16[32,16,1152]{2,1,0:T(8,128)(2,1)} all-to-all(bf16[32,16,1152]{2,1,0:T(8,128)(2,1)} %update.2), channel_id=1, replica_groups=mesh['freq'=32,'rec'=8] {'freq'}, dimensions={0} | all-to-all | bytes 2359296 | tf_op jit(solution)/shard_map/all_to_all | solution.py:257
  195.0 6.9 %product.3 = bf16[8,128,128]{2,1,0:T(8,128)(2,1)} custom-call(bf16[2,4,256,1152]{3,2,1,0:T(8,128)(2,1)} %k_ref.7, bf16[32,16,1152]{2,1,0:T(8,128)(2,1)} %all_to_all.42.x_ref, bf16[512,512]{1,0:T(8,128)(2,1)} %constant.17.clone.order_ref, bf16[128,128]{1,0:T(8,128)(2,1)} %constant.18.clone.pairs_ref), custom_call_target="tpu_custom_call" | custom-call | flops 603979776 | bytes 5898240 | tf_op jit(solution)/shard_map/product/pallas_call | solution.py:107
  201.9 23.1 %all_to_all.43 = bf16[256,4,128]{2,1,0:T(4,128)(2,1)} all-to-all(bf16[256,4,128]{2,1,0:T(4,128)(2,1)} %bitcast.16), channel_id=1, replica_groups=mesh['freq'=32,'rec'=8] {'rec','freq'}, dimensions={0} | all-to-all | bytes 524288 | tf_op jit(solution)/shard_map/all_to_all | solution.py:257
  225.0 3.3 %source.3 = (bf16[128,128]{1,0:T(8,128)(2,1)}, bf16[2,32,1024]{2,1,0:T(8,128)(2,1)}) custom-call(bf16[8,128,128]{2,1,0:T(8,128)(2,1)} %bitcast.20, s32[2,32,1]{2,1,0:T(8,128)} %copy.11.onset_ref, bf16[256,1024]{1,0:T(8,128)(2,1)} %constant.16.clone.table_ref), custom_call_target="tpu_custom_call" | custom-call | flops 536870912 | bytes 524288 | tf_op jit(solution)/shard_map/source/pallas_call | solution.py:164
  228.3 0.8 broadcast_in_dim.25
  229.1 21.3 %all_to_all.44 = bf16[256,4,128]{2,1,0:T(4,128)(2,1)} all-to-all(bf16[256,4,128]{2,1,0:T(4,128)(2,1)S(1)} %bitcast.18), channel_id=1, replica_groups=mesh['freq'=32,'rec'=8] {'rec','freq'}, dimensions={0} | all-to-all | bytes 524288 | tf_op jit(solution)/shard_map/all_to_all | solution.py:257
  250.4 6.3 %adjoint.3 = bf16[32,16,1152]{2,1,0:T(8,128)(2,1)} custom-call(bf16[2,4,256,1152]{3,2,1,0:T(8,128)(2,1)} %k_ref.7, bf16[8,128,128]{2,1,0:T(8,128)(2,1)} %bitcast.14, bf16[128,128]{1,0:T(8,128)(2,1)} %constant.18.clone.pairs_ref, bf16[512,512]{1,0:T(8,128)(2,1)} %constant.17.clone.order_ref), custom_call_target="tpu_custom_call" | custom-call | flops 603979776 | bytes 5898240 | tf_op jit(solution)/shard_map/adjoint/pallas_call | solution.py:200
  256.7 37.4 %all_to_all.45.q_ref = bf16[32,16,1152]{2,1,0:T(8,128)(2,1)} all-to-all(bf16[32,16,1152]{2,1,0:T(8,128)(2,1)} %adjoint.3), channel_id=1, replica_groups=mesh['freq'=32,'rec'=8] {'freq'}, dimensions={0} | all-to-all | bytes 2359296 | tf_op jit(solution)/shard_map/all_to_all | solution.py:257
  294.2 7.4 %update.3 = bf16[2,1152,1024]{2,1,0:T(8,128)(2,1)} custom-call(bf16[32,16,1152]{2,1,0:T(8,128)(2,1)} %all_to_all.45.q_ref, bf16[2,1152,1024]{2,1,0:T(8,128)(2,1)} %f_ref.5, s32[2,1152,1]{2,1,0:T(8,128)} %copy.12.onset_ref, bf16[256,1024]{1,0:T(8,128)(2,1)} %constant.16.clone.table_ref), custom_call_target="tpu_custom_call" | custom-call | flops 2415919104 | bytes 10616832 | tf_op jit(solution)/shard_map/update/pallas_call | solution.py:245
Async XLA Ops:
  0.6 64.7 %copy-start = (s32[2,256]{1,0:T(2,128)S(1)}, s32[2,256]{1,0:T(2,128)}, u32[]{:S(2)}) copy-start(s32[2,256]{1,0:T(2,128)} %param.9) | copy-start | bytes 6148
  58.3 22.6 %all-to-all-start.1 = ((bf16[256,4,128]{2,1,0:T(4,128)(2,1)}), bf16[256,4,128]{2,1,0:T(4,128)(2,1)S(1)}, u32[]{:S(2)}, u32[]{:S(2)}) async-start(bf16[256,4,128]{2,1,0:T(4,128)(2,1)} %bitcast.13), calls=%async_computation.1 | async-start | bytes 524288 | tf_op jit(solution)/shard_map/all_to_all | solution.py:257
  80.8 0.7 copy-start.2
  113.3 4.2 %copy-start.3 = (s32[2,1152]{1,0:T(2,128)S(1)}, s32[2,1152]{1,0:T(2,128)}, u32[]{:S(2)}) copy-start(s32[2,1152]{1,0:T(2,128)} %param.10) | copy-start | bytes 27652
  113.3 35.0 %all-to-all-start.3 = ((bf16[32,16,1152]{2,1,0:T(8,128)(2,1)}), bf16[32,16,1152]{2,1,0:T(8,128)(2,1)S(1)}, u32[]{:S(2)}, u32[]{:S(2)}) async-start(bf16[32,16,1152]{2,1,0:T(8,128)(2,1)} %adjoint.2), calls=%async_computation.3 | async-start | bytes 2359296 | tf_op jit(solution)/shard_map/all_to_all | solution.py:257
  148.3 1.0 copy-start.1

commit v2 on v1

v2 whole, which is shorter than its diff:
```python
import functools

import jax
import jax.numpy as jnp
import numpy as np
from jax import lax
from jax.experimental import pallas as pl
from jax.experimental.pallas import tpu as pltpu
from jax.sharding import PartitionSpec as P

LOW = 8
ITERS = 2
F32 = jnp.float32
BF16 = jnp.bfloat16
NN = (((1,), (0,)), ((), ()))
NT = (((1,), (1,)), ((), ()))
TN = (((0,), (0,)), ((), ()))


def dot(a, b, dims=NN):
    return lax.dot_general(a, b, dims, preferred_element_type=F32)


def make_table(freq, own, samples):
    k = np.arange(freq * own)[:, None] + LOW
    t = np.arange(samples)[None, :]
    phase = ((k * t) % samples).astype(np.float32) * np.float32(2.0 * 3.141592653589793 / samples)
    both = np.stack([np.cos(phase), -np.sin(phase)]).astype(np.float32)
    rows = both.reshape(2, freq, own, samples).transpose(1, 0, 2, 3)
    return jnp.asarray(rows.reshape(freq * 2 * own, samples), BF16)


def make_order(freq, points, own):
    n = freq * points * 2 * own
    rows = np.arange(n).reshape(freq, points, 2, own).transpose(3, 2, 0, 1).reshape(n)
    return jnp.asarray(np.eye(n, dtype=np.float32)[rows], BF16)


def make_pairs(freq, points):
    n = freq * points * 2
    rows = np.arange(n).reshape(2, freq, points).transpose(1, 2, 0).reshape(n)
    return jnp.asarray(np.eye(n, dtype=np.float32)[rows], BF16)


VSPEC = pl.BlockSpec(memory_space=pltpu.VMEM)
ANY = pl.BlockSpec(memory_space=pl.ANY)
PARAMS = pltpu.CompilerParams(vmem_limit_bytes=24 << 20)


def vmem(x):
    return pltpu.with_memory_space_constraint(x, pltpu.VMEM)


def hbm(x):
    return pltpu.with_memory_space_constraint(x, pltpu.HBM)


def vout(shape):
    return pltpu.VMEM(shape, BF16)


def cost(flops, bytes_accessed):
    return pl.CostEstimate(flops=int(flops), transcendentals=0, bytes_accessed=int(bytes_accessed))


def pieces(length, size):
    return [slice(at, min(at + size, length)) for at in range(0, length, size)]


def spectrum_kernel(f_hbm, table_hbm, out_ref, f_buf, table_buf, sems):
    freq = out_ref.shape[0]
    points, receivers, _ = f_buf.shape
    ats = pieces(receivers, 256)
    copies = [pltpu.make_async_copy(f_hbm.at[:, at], f_buf.at[:, at], sems.at[i]) for i, at in enumerate(ats)]
    table_copy = pltpu.make_async_copy(table_hbm, table_buf, sems.at[len(ats)])
    table_copy.start()
    copies[0].start()
    table_copy.wait()
    copies[1].start()
    for i, at in enumerate(ats):
        copies[i].wait()
        if i + 2 < len(ats):
            copies[i + 2].start()
        parts = [dot(table_buf[...], f_buf[p, at], NT) for p in range(points)]
        parts = [s.reshape(freq, s.shape[0] // freq, s.shape[1]) for s in parts]
        out_ref[:, :, at] = jnp.concatenate(parts, axis=1).astype(BF16)


def spectrum(f, table, freq):
    points, receivers, _ = f.shape
    rows = points * table.shape[0] // freq
    return pl.pallas_call(
        spectrum_kernel,
        in_specs=[ANY, ANY],
        out_specs=VSPEC,
        out_shape=jax.ShapeDtypeStruct((freq, rows, receivers), BF16),
        scratch_shapes=[
            pltpu.VMEM(f.shape, BF16),
            pltpu.VMEM(table.shape, BF16),
            pltpu.SemaphoreType.DMA((len(pieces(receivers, 256)) + 1,)),
        ],
        compiler_params=PARAMS,
        cost_estimate=cost(2 * f.size * table.shape[0], 2 * (f.size + freq * rows * receivers)),
        name="spectrum",
    )(hbm(f), hbm(table))


def product_kernel(k_hbm, x_ref, order_ref, pairs_ref, late_ref, out_ref, k_buf, w, sems):
    own, rows, receivers = w.shape
    half = rows // 2
    blocks, _, width = out_ref.shape
    share = width // own
    copies = [pltpu.make_async_copy(k_hbm.at[:, kk], k_buf.at[:, kk], sems.at[kk]) for kk in range(own)]
    for copy in copies[:2]:
        copy.start()
    x = x_ref[...].reshape(own * rows, receivers)
    w[...] = dot(order_ref[...], x).astype(BF16).reshape(w.shape)
    g = []
    for kk in range(own):
        w0 = w[kk]
        w1 = jnp.concatenate([-w0[half:], w0[:half]], axis=0)
        copies[kk].wait()
        if kk + 2 < own:
            copies[kk + 2].start()
        total = dot(k_buf[0, kk], w0, NT) + dot(k_buf[1, kk], w1, NT)
        g.append(dot(pairs_ref[...], total.astype(BF16), NT))
    for j in range(blocks):
        parts = [g[kk][:, j * share : (j + 1) * share] for kk in range(own)]
        out_ref[j] = jnp.concatenate(parts, axis=1).astype(BF16)


def product(kernel, x, order, pairs, late, blocks):
    _, own, sources, receivers = kernel.shape
    rows = order.shape[0] // own
    width = own * sources // blocks
    return pl.pallas_call(
        product_kernel,
        in_specs=[ANY, VSPEC, VSPEC, VSPEC, ANY],
        out_specs=[VSPEC, VSPEC],
        out_shape=[vout((blocks, rows, width)), vout(kernel.shape)],
        scratch_shapes=[pltpu.VMEM((own, rows, receivers), BF16), pltpu.SemaphoreType.DMA((own,))],
        compiler_params=PARAMS,
        cost_estimate=cost(2 * kernel.size * rows, 2 * (kernel.size + x.size)),
        name="product",
    )(hbm(kernel), vmem(x), vmem(order), vmem(pairs), late)


def source_kernel(points, keep_field, v_ref, onset_ref, table_ref, h_ref, *field_ref):
    rows, samples = table_ref.shape
    copies, lines, width = h_ref.shape
    share = onset_ref.shape[1]
    own = width // share
    table = table_ref[...]
    v = v_ref[...].astype(F32)
    if v.ndim == 3:
        v = jnp.sum(v, axis=0)
    v = v.astype(BF16)
    row = lax.broadcasted_iota(jnp.int32, (rows, lines), 0)
    line = lax.broadcasted_iota(jnp.int32, (rows, lines), 1)
    device, part, mine = row // (2 * own), row // own % 2, row % own
    h = [jnp.zeros((lines, share), F32) for _ in range(own)]
    for p in range(points):
        at = (device * points + p) * 2 + part
        picks = [jnp.where((line == at) & (mine == kk), 1.0, 0.0).astype(BF16) for kk in range(own)]
        full = jnp.zeros((rows, share), F32)
        for kk in range(own):
            full = full + dot(picks[kk], v[:, kk * share : (kk + 1) * share])
        g = dot(full.astype(BF16), table, TN) * (2.0 / samples)
        if keep_field:
            field_ref[0][p] = g.astype(BF16)
        times = lax.broadcasted_iota(jnp.int32, g.shape, 1)
        muted = jnp.where(times < onset_ref[p], g, 0.0).astype(BF16)
        back = dot(table, muted, NT).astype(BF16)
        for kk in range(own):
            h[kk] = h[kk] + dot(picks[kk], back, TN)
    full = jnp.concatenate(h, axis=1).astype(BF16)
    for j in range(copies):
        h_ref[j] = full


def source_step(v, onset, table, keep_field, copies):
    samples = table.shape[1]
    points, share, _ = onset.shape
    out_shape = [vout((copies,) + v.shape[-2:])]
    if keep_field:
        out_shape.append(jax.ShapeDtypeStruct((points, share, samples), BF16))
    return pl.pallas_call(
        functools.partial(source_kernel, points, keep_field),
        in_specs=[VSPEC] * 3,
        out_specs=[VSPEC] * len(out_shape),
        out_shape=out_shape,
        compiler_params=PARAMS,
        cost_estimate=cost(4 * v.size * samples, 2 * table.size),
        name="source",
    )(vmem(v), vmem(onset), vmem(table))


def adjoint_kernel(k_ref, u_ref, pairs_ref, order_ref, out_ref, o):
    own, rows, receivers = o.shape
    half = rows // 2
    blocks, _, width = u_ref.shape
    share = width // own
    for kk in range(own):
        parts = [u_ref[j, :, kk * share : (kk + 1) * share] for j in range(blocks)]
        l0 = dot(pairs_ref[...], jnp.concatenate(parts, axis=1), TN).astype(BF16)
        l1 = jnp.concatenate([l0[half:], -l0[:half]], axis=0)
        o[kk] = (dot(l0, k_ref[0, kk]) + dot(l1, k_ref[1, kk])).astype(BF16)
    flat = o[...].reshape(own * rows, receivers)
    out_ref[...] = dot(order_ref[...], flat, TN).astype(BF16).reshape(out_ref.shape)


def adjoint(kernel, u, pairs, order, freq):
    _, own, sources, receivers = kernel.shape
    rows = u.shape[1]
    return pl.pallas_call(
        adjoint_kernel,
        in_specs=[VSPEC] * 4,
        out_specs=VSPEC,
        out_shape=jax.ShapeDtypeStruct((freq, own * rows // freq, receivers), BF16),
        scratch_shapes=[pltpu.VMEM((own, rows, receivers), BF16)],
        compiler_params=PARAMS,
        cost_estimate=cost(2 * kernel.size * rows, 2 * own * rows * receivers),
        name="adjoint",
    )(vmem(kernel), vmem(u), vmem(pairs), vmem(order))


def after_kernel(x_ref, late_ref, out_ref):
    out_ref[...] = x_ref[...]


def after(x, late):
    return pl.pallas_call(
        after_kernel,
        in_specs=[VSPEC, ANY],
        out_specs=VSPEC,
        out_shape=jax.ShapeDtypeStruct(x.shape, x.dtype),
        compiler_params=PARAMS,
        cost_estimate=cost(x.size, 8 * x.size),
        name="after",
    )(x, late)


def own_rows(q, points, p, scale):
    freq, rows, block = q.shape
    each = rows // points
    mine = q.astype(F32)[:, p * each : (p + 1) * each] * scale
    return mine.reshape(freq * each, block).astype(BF16)


def respectrum_kernel(block, q_ref, first_hbm, onset_ref, table_ref, across_ref, out_ref, first_ref, sem):
    copy = pltpu.make_async_copy(first_hbm, first_ref, sem)
    copy.start()
    freq, rows, receivers = q_ref.shape
    samples, _ = across_ref.shape
    points = onset_ref.shape[0]
    for i, at in enumerate(pieces(receivers, block)):
        wide = at.stop - at.start
        times = lax.broadcasted_iota(jnp.int32, (samples, wide), 0)
        parts = []
        for p in range(points):
            q = dot(across_ref[...], own_rows(q_ref[:, :, at], points, p, 2.0 / samples))
            muted = jnp.where(times < onset_ref[p, :, at], q, 0.0).astype(BF16)
            parts.append(dot(table_ref[...], muted).reshape(freq, rows // points, wide))
        if i == 0:
            copy.wait()
        out_ref[:, :, at] = (first_ref[:, :, at].astype(F32) + jnp.concatenate(parts, axis=1)).astype(BF16)


def respectrum(q, first, onset, table, across, block=512):
    freq, rows, receivers = q.shape
    return pl.pallas_call(
        functools.partial(respectrum_kernel, block),
        in_specs=[VSPEC, ANY, VSPEC, VSPEC, VSPEC],
        out_specs=VSPEC,
        out_shape=jax.ShapeDtypeStruct(q.shape, BF16),
        scratch_shapes=[pltpu.VMEM(q.shape, BF16), pltpu.SemaphoreType.DMA],
        compiler_params=PARAMS,
        cost_estimate=cost(4 * q.size * table.shape[1], 6 * q.size),
        name="respectrum",
    )(vmem(q), hbm(first), vmem(onset), vmem(table), vmem(across))


def update_kernel(q_ref, f_ref, onset_ref, table_ref, out_ref):
    points, block, samples = f_ref.shape
    at = pl.ds(pl.program_id(0) * block, block)
    times = lax.broadcasted_iota(jnp.int32, (block, samples), 1)
    for p in range(points):
        q = dot(own_rows(q_ref[:, :, at], points, p, 2.0 / samples), table_ref[...], TN)
        out_ref[p] = (f_ref[p].astype(F32) + jnp.where(times < onset_ref[p], q, 0.0)).astype(BF16)


def update(q, f, onset, table, block=384):
    points, receivers, samples = f.shape
    trace_block = pl.BlockSpec((points, block, samples), lambda i: (0, i, 0))
    return pl.pallas_call(
        update_kernel,
        grid=(receivers // block,),
        in_specs=[VSPEC, trace_block, pl.BlockSpec((points, block, 1), lambda i: (0, i, 0)), VSPEC],
        out_specs=trace_block,
        out_shape=jax.ShapeDtypeStruct(f.shape, BF16),
        compiler_params=PARAMS,
        cost_estimate=cost(2 * f.size * table.shape[0], 2 * (2 * f.size + q.size)),
        name="update",
    )(vmem(q), f, onset, vmem(table))


def exchange(x, axis):
    return lax.all_to_all(x, axis, split_axis=0, concat_axis=0, tiled=True)


def body(kernel, focusing_in, onset_src, onset_rec):
    freq = lax.axis_size("freq")
    rec = lax.axis_size("rec")
    _, own, sources, receivers = kernel.shape
    points, _, samples = focusing_in.shape
    share = sources // rec
    lines, width = freq * points * 2, own * share
    table = make_table(freq, own, samples)
    order = make_order(freq, points, own)
    pairs = make_pairs(freq, points)
    start = spec = spectrum(focusing_in, table, freq)
    own_sources = lax.dynamic_slice_in_dim(after(onset_src, start), lax.axis_index("rec") * share, share, 1)
    late = src_onsets = own_sources[:, :, None]
    for step in range(ITERS):
        last = step == ITERS - 1
        part, held = product(kernel, exchange(spec, "freq"), order, pairs, late, rec)
        v = exchange(part.reshape(rec * freq, points * 2, width), ("rec", "freq")).reshape(rec, lines, width)
        h, *field = source_step(v, src_onsets, table, last, rec)
        u = exchange(h.reshape(rec * freq, points * 2, width), ("rec", "freq")).reshape(rec, lines, width)
        q = adjoint(held, u, pairs, order, freq)
        if last:
            return update(exchange(q, "freq"), focusing_in, late, table), field[0]
        row, across = after(onset_rec, q)[:, None, :], lax.optimization_barrier(table).T
        spec = respectrum(exchange(q, "freq"), start, row, table, across)
        late = after(onset_rec, spec)[:, :, None]


def solution(mesh):
    placed = (
        P(None, "freq", None, "rec"),
        P("freq", "rec", None),
        P("freq", None),
        P("freq", "rec"),
    )
    return jax.shard_map(
        body,
        mesh=mesh,
        in_specs=placed,
        out_specs=(P("freq", "rec", None), P("freq", "rec", None)),
        check_vma=False,
    )
```

time: 303 us -> 274 us (0.904)
  blocking collectives: 187 us -> 125 us
  waiting for transfers between devices: 44.1 us -> 91.4 us
  Pallas kernels: 52.6 us -> 32.1 us
  starting transfers between devices: 11.2 us -> 22.9 us
  local copies, waits for them, and re-layouts: 5.63 us -> 0.82 us
    all_to_all x6 -> x5, blocking collectives: 187 us -> 125 us  [exchange(): return lax.all_to_all(x, axis, split_axis=0, concat_axis=0, tiled=True)]
    all_to_all x2 -> x3, waiting for transfers between devices: 44.1 us -> 91.4 us  [exchange(): return lax.all_to_all(x, axis, split_axis=0, concat_axis=0, tiled=True)]
    pallas_call x9 -> x12, Pallas kernels: 52.6 us -> 32.1 us  [the longest x2 8.52 us: product(): pl.pallas_call(product_kernel, in_specs=[ANY, VSPEC, VSPEC, VSPEC, ANY],...]
    all_to_all x2 -> x3, starting transfers between devices: 11.2 us -> 22.9 us  [exchange(): return lax.all_to_all(x, axis, split_axis=0, concat_axis=0, tiled=True)]
    broadcast_in_dim x5 -> x4, local copies, waits for them, and re-layouts: 3.9 us -> 0.58 us  [the longest x1 0.4 us: body(): late = after(onset_rec, spec)[:, :, None]]
  transfers between devices with their start and end apart: 2 -> 3, of which waited for: 2 -> 3; matrix products, arithmetic and copies ran while one was open for 1% -> 0% of each run, Pallas kernels for 0% -> 0%
where the time goes in v2:
time: 274 us; the launch traced here: 273 us
  blocking collectives  125 us (46%)
  waiting for transfers between devices  91.4 us (33%)
  Pallas kernels  32.1 us (12%)
  starting transfers between devices  22.9 us (8%)
    all_to_all x5, blocking collectives, exchange(): return lax.all_to_all(x, axis, split_axis=0, concat_axis=0, tiled=True)  125 us
    all_to_all x3, waiting for transfers between devices, exchange(): return lax.all_to_all(x, axis, split_axis=0, concat_axis=0, tiled=True)  91.4 us
    all_to_all x3, starting transfers between devices, exchange(): return lax.all_to_all(x, axis, split_axis=0, concat_axis=0, tiled=True)  22.9 us
    pallas_call x2, Pallas kernels, product(): pl.pallas_call(product_kernel, in_specs=[ANY, VSPEC, VSPEC, VSPEC, ANY],...  8.52 us
    pallas_call x1, Pallas kernels, spectrum(): pl.pallas_call(spectrum_kernel, in_specs=[ANY, ANY], out_specs=VSPEC, out...  5.63 us
    pallas_call x2, Pallas kernels, adjoint(): pl.pallas_call(adjoint_kernel, in_specs=[VSPEC] * 4, out_specs=VSPEC, out...  5.59 us
  transfers between devices with their start and end apart: 3, of which 3 were waited for; matrix products, arithmetic and copies ran while one was open for 0% of the time, Pallas kernels for 0%

profile of v2, /device:TPU:1, one launch (start us, length us, event | category | flops | bytes accessed | tf_op | source)
XLA Modules:
  0.0 273.0 jit_solution(1673021023777132351)
XLA Ops:
  0.6 5.6 %spectrum.1.late_ref.first_hbm = bf16[32,16,1152]{2,1,0:T(8,128)(2,1)} custom-call(bf16[2,1152,1024]{2,1,0:T(8,128)(2,1)} %f_ref.1, bf16[256,1024]{1,0:T(8,128)(2,1)} %constant.16.clone.table_hbm.table_ref), custom_call_target="tpu_custom_call" | custom-call | flops 1207959552 | bytes 5898240 | tf_op jit(solution)/shard_map/spectrum/pallas_call | solution.py:92
  6.3 0.0 copy-start.4
  6.3 12.6 %all-to-all-start = ((bf16[32,16,1152]{2,1,0:T(8,128)(2,1)}), bf16[32,16,1152]{2,1,0:T(8,128)(2,1)S(1)}, u32[]{:S(2)}, u32[]{:S(2)}) async-start(bf16[32,16,1152]{2,1,0:T(8,128)(2,1)} %spectrum.1.late_ref.first_hbm), calls=%async_computation | async-start | bytes 2359296 | tf_op jit(solution)/shard_map/all_to_all | solution.py:308
  18.9 0.0 copy-done.4
  18.9 0.0 copy-start
  18.9 0.0 copy-start.2
  18.9 0.1 dynamic-slice_bitcast_fusion
  19.0 0.1 copy.13.late_ref.onset_ref
  19.1 0.0 copy-start.1
  19.1 30.6 %all-to-all-done.x_ref = bf16[32,16,1152]{2,1,0:T(8,128)(2,1)S(1)} async-done(((bf16[32,16,1152]{2,1,0:T(8,128)(2,1)}), bf16[32,16,1152]{2,1,0:T(8,128)(2,1)S(1)}, u32[]{:S(2)}, u32[]{:S(2)}) %all-to-all-start) | async-done | bytes 1179680 | tf_op jit(solution)/shard_map/all_to_all | solution.py:308
  49.7 0.0 copy-done
  49.7 0.0 copy-done.2
  49.7 4.3 %product.2 = (bf16[8,128,128]{2,1,0:T(8,128)(2,1)S(1)}, bf16[2,4,256,1152]{3,2,1,0:T(8,128)(2,1)S(1)}) custom-call(bf16[2,4,256,1152]{3,2,1,0:T(8,128)(2,1)} %k_hbm.3, bf16[32,16,1152]{2,1,0:T(8,128)(2,1)S(1)} %all-to-all-done.x_ref, bf16[512,512]{1,0:T(8,128)(2,1)S(1)} %copy-done, bf16[128,128]{1,0:T(8,128)(2,1)S(1)} %copy-done.2, ...), custom_call_target="tpu_custom_call" | custom-call | flops 603979776 | bytes 5898240 | tf_op jit(solution)/shard_map/product/pallas_call | solution.py:136
  54.0 24.3 %all_to_all.40 = bf16[256,4,128]{2,1,0:T(4,128)(2,1)S(1)} all-to-all(bf16[256,4,128]{2,1,0:T(4,128)(2,1)S(1)} %bitcast.19), channel_id=1, replica_groups=mesh['freq'=32,'rec'=8] {'rec','freq'}, dimensions={0} | all-to-all | bytes 524288 | tf_op jit(solution)/shard_map/all_to_all | solution.py:308
  78.3 0.0 copy-done.1
  78.3 1.5 source.2
  79.8 20.6 %all_to_all.41 = bf16[256,4,128]{2,1,0:T(4,128)(2,1)S(1)} all-to-all(bf16[256,4,128]{2,1,0:T(4,128)(2,1)S(1)} %bitcast.22), channel_id=1, replica_groups=mesh['freq'=32,'rec'=8] {'rec','freq'}, dimensions={0} | all-to-all | bytes 524288 | tf_op jit(solution)/shard_map/all_to_all | solution.py:308
  100.4 3.3 %adjoint.2.late_ref = bf16[32,16,1152]{2,1,0:T(8,128)(2,1)} custom-call(bf16[2,4,256,1152]{3,2,1,0:T(8,128)(2,1)S(1)} %get-tuple-element.8.k_ref, bf16[8,128,128]{2,1,0:T(8,128)(2,1)S(1)} %bitcast.16, bf16[128,128]{1,0:T(8,128)(2,1)S(1)} %copy-done.2, bf16[512,512]{1,0:T(8,128)(2,1)S(1)} %copy-done), custom_call_target="tpu_custom_call" | custom-call | flops 603979776 | bytes 1179648 | tf_op jit(solution)/shard_map/adjoint/pallas_call | solution.py:215
  103.7 0.0 copy-start.3
  103.7 4.2 %all-to-all-start.3 = ((bf16[32,16,1152]{2,1,0:T(8,128)(2,1)}), bf16[32,16,1152]{2,1,0:T(8,128)(2,1)S(1)}, u32[]{:S(2)}, u32[]{:S(2)}) async-start(bf16[32,16,1152]{2,1,0:T(8,128)(2,1)} %adjoint.2.late_ref), calls=%async_computation.3 | async-start | bytes 2359296 | tf_op jit(solution)/shard_map/all_to_all | solution.py:308
  107.9 0.2 copy.15.across_ref
  108.1 0.0 copy-done.3
  108.2 30.3 %all-to-all-done.3.q_ref = bf16[32,16,1152]{2,1,0:T(8,128)(2,1)S(1)} async-done(((bf16[32,16,1152]{2,1,0:T(8,128)(2,1)}), bf16[32,16,1152]{2,1,0:T(8,128)(2,1)S(1)}, u32[]{:S(2)}, u32[]{:S(2)}) %all-to-all-start.3) | async-done | bytes 1179680 | tf_op jit(solution)/shard_map/all_to_all | solution.py:308
  138.5 4.6 %respectrum.1.late_ref = bf16[32,16,1152]{2,1,0:T(8,128)(2,1)} custom-call(bf16[32,16,1152]{2,1,0:T(8,128)(2,1)S(1)} %all-to-all-done.3.q_ref, bf16[32,16,1152]{2,1,0:T(8,128)(2,1)} %spectrum.1.late_ref.first_hbm, s32[2,1,1152]{2,1,0:T(1,128)S(1)} %broadcast_in_dim.10.onset_ref, bf16[256,1024]{1,0:T(8,128)(2,1)S(1)} %copy-done.1, ...), custom_call_target="tpu_custom_call" | custom-call | flops 2415919104 | bytes 3538944 | tf_op jit(solution)/shard_map/respectrum/pallas_call | solution.py:271
  143.1 6.1 %all-to-all-start.4 = ((bf16[32,16,1152]{2,1,0:T(8,128)(2,1)}), bf16[32,16,1152]{2,1,0:T(8,128)(2,1)S(1)}, u32[]{:S(2)}, u32[]{:S(2)}) async-start(bf16[32,16,1152]{2,1,0:T(8,128)(2,1)} %respectrum.1.late_ref), calls=%async_computation.4 | async-start | bytes 2359296 | tf_op jit(solution)/shard_map/all_to_all | solution.py:308
  149.3 0.4 copy.16.late_ref.onset_ref
  149.7 30.4 %all-to-all-done.4.x_ref = bf16[32,16,1152]{2,1,0:T(8,128)(2,1)S(1)} async-done(((bf16[32,16,1152]{2,1,0:T(8,128)(2,1)}), bf16[32,16,1152]{2,1,0:T(8,128)(2,1)S(1)}, u32[]{:S(2)}, u32[]{:S(2)}) %all-to-all-start.4) | async-done | bytes 1179680 | tf_op jit(solution)/shard_map/all_to_all | solution.py:308
  180.1 4.3 %product.3 = (bf16[8,128,128]{2,1,0:T(8,128)(2,1)S(1)}, bf16[2,4,256,1152]{3,2,1,0:T(8,128)(2,1)S(1)}) custom-call(bf16[2,4,256,1152]{3,2,1,0:T(8,128)(2,1)} %k_hbm.3, bf16[32,16,1152]{2,1,0:T(8,128)(2,1)S(1)} %all-to-all-done.4.x_ref, bf16[512,512]{1,0:T(8,128)(2,1)S(1)} %copy-done, bf16[128,128]{1,0:T(8,128)(2,1)S(1)} %copy-done.2, ...), custom_call_target="tpu_custom_call" | custom-call | flops 603979776 | bytes 5898240 | tf_op jit(solution)/shard_map/product/pallas_call | solution.py:136
  184.4 22.8 %all_to_all.42 = bf16[256,4,128]{2,1,0:T(4,128)(2,1)S(1)} all-to-all(bf16[256,4,128]{2,1,0:T(4,128)(2,1)S(1)} %bitcast.20), channel_id=1, replica_groups=mesh['freq'=32,'rec'=8] {'rec','freq'}, dimensions={0} | all-to-all | bytes 524288 | tf_op jit(solution)/shard_map/all_to_all | solution.py:308
  207.3 0.0 slice-start
  207.3 2.0 source.3
  209.3 20.6 %all_to_all.43 = bf16[256,4,128]{2,1,0:T(4,128)(2,1)S(1)} all-to-all(bf16[256,4,128]{2,1,0:T(4,128)(2,1)S(1)} %bitcast.18), channel_id=1, replica_groups=mesh['freq'=32,'rec'=8] {'rec','freq'}, dimensions={0} | all-to-all | bytes 524288 | tf_op jit(solution)/shard_map/all_to_all | solution.py:308
  229.9 0.0 slice-start.1
  229.9 2.3 adjoint.3
  232.2 36.6 %all_to_all.44.q_ref = bf16[32,16,1152]{2,1,0:T(8,128)(2,1)S(1)} all-to-all(bf16[32,16,1152]{2,1,0:T(8,128)(2,1)S(1)} %adjoint.3), channel_id=1, replica_groups=mesh['freq'=32,'rec'=8] {'freq'}, dimensions={0} | all-to-all | bytes 2359296 | tf_op jit(solution)/shard_map/all_to_all | solution.py:308
  268.8 0.0 slice-done
  268.8 0.0 slice-done.1
  268.8 4.2 %update.1 = bf16[2,1152,1024]{2,1,0:T(8,128)(2,1)} custom-call(bf16[32,16,1152]{2,1,0:T(8,128)(2,1)S(1)} %all_to_all.44.q_ref, bf16[2,1152,1024]{2,1,0:T(8,128)(2,1)S(1)} %bitcast.13, s32[2,1152,1]{2,1,0:T(8,128)S(1)} %copy.16.late_ref.onset_ref, bf16[256,1024]{1,0:T(8,128)(2,1)S(1)} %copy-done.1), custom_call_target="tpu_custom_call" | custom-call | flops 1207959552 | bytes 10616832 | tf_op jit(solution)/shard_map/update/pallas_call | solution.py:295
  (5 shorter events, 0.0 us)
Async XLA Ops:
  6.3 12.6 %copy-start.4 = (s32[2,256]{1,0:T(2,128)S(1)}, s32[2,256]{1,0:T(2,128)}, u32[]{:S(2)}) copy-start(s32[2,256]{1,0:T(2,128)} %x_ref.3) | copy-start | bytes 6148
  6.3 43.4 %all-to-all-start = ((bf16[32,16,1152]{2,1,0:T(8,128)(2,1)}), bf16[32,16,1152]{2,1,0:T(8,128)(2,1)S(1)}, u32[]{:S(2)}, u32[]{:S(2)}) async-start(bf16[32,16,1152]{2,1,0:T(8,128)(2,1)} %spectrum.1.late_ref.first_hbm), calls=%async_computation | async-start | bytes 2359296 | tf_op jit(solution)/shard_map/all_to_all | solution.py:308
  18.9 30.8 %copy-start = (bf16[512,512]{1,0:T(8,128)(2,1)S(1)}, bf16[512,512]{1,0:T(8,128)(2,1)}, u32[]{:S(2)}) copy-start(bf16[512,512]{1,0:T(8,128)(2,1)} %constant.17.clone.order_ref) | copy-start | bytes 1572868
  18.9 30.8 %copy-start.2 = (bf16[128,128]{1,0:T(8,128)(2,1)S(1)}, bf16[128,128]{1,0:T(8,128)(2,1)}, u32[]{:S(2)}) copy-start(bf16[128,128]{1,0:T(8,128)(2,1)} %constant.18.clone.pairs_ref) | copy-start | bytes 98308
  19.1 59.2 %copy-start.1 = (bf16[256,1024]{1,0:T(8,128)(2,1)S(1)}, bf16[256,1024]{1,0:T(8,128)(2,1)}, u32[]{:S(2)}) copy-start(bf16[256,1024]{1,0:T(8,128)(2,1)} %constant.16.clone.table_hbm.table_ref) | copy-start | bytes 1572868
  103.7 4.4 %copy-start.3 = (s32[2,1152]{1,0:T(2,128)S(1)}, s32[2,1152]{1,0:T(2,128)}, u32[]{:S(2)}) copy-start(s32[2,1152]{1,0:T(2,128)} %x_ref.5) | copy-start | bytes 27652
  103.7 34.7 %all-to-all-start.3 = ((bf16[32,16,1152]{2,1,0:T(8,128)(2,1)}), bf16[32,16,1152]{2,1,0:T(8,128)(2,1)S(1)}, u32[]{:S(2)}, u32[]{:S(2)}) async-start(bf16[32,16,1152]{2,1,0:T(8,128)(2,1)} %adjoint.2.late_ref), calls=%async_computation.3 | async-start | bytes 2359296 | tf_op jit(solution)/shard_map/all_to_all | solution.py:308
  143.1 37.0 %all-to-all-start.4 = ((bf16[32,16,1152]{2,1,0:T(8,128)(2,1)}), bf16[32,16,1152]{2,1,0:T(8,128)(2,1)S(1)}, u32[]{:S(2)}, u32[]{:S(2)}) async-start(bf16[32,16,1152]{2,1,0:T(8,128)(2,1)} %respectrum.1.late_ref), calls=%async_computation.4 | async-start | bytes 2359296 | tf_op jit(solution)/shard_map/all_to_all | solution.py:308
  207.3 61.5 %slice-start = ((s8[4718592]{0:T(1024)(128)(4,1)}), s8[4194304]{0:T(1024)(128)(4,1)S(1)}, s32[]{:S(2)}) async-start(s8[4718592]{0:T(1024)(128)(4,1)} %bitcast.12), calls=%async_computation.8 | async-start | bytes 8388608
  229.9 38.9 %slice-start.1 = ((s8[4718592]{0:T(1024)(128)(4,1)}), s8[524288]{0:T(1024)(128)(4,1)S(1)}, s32[]{:S(2)}) async-start(s8[4718592]{0:T(1024)(128)(4,1)} %bitcast.12), calls=%async_computation.9 | async-start | bytes 1048576

commit v3 on v2

--- a/solution.py
+++ b/solution.py
@@ -63,14 +63,20 @@
     return pl.CostEstimate(flops=int(flops), transcendentals=0, bytes_accessed=int(bytes_accessed))
 
 
-def pieces(length, size):
-    return [slice(at, min(at + size, length)) for at in range(0, length, size)]
-
-
-def spectrum_kernel(f_hbm, table_hbm, out_ref, f_buf, table_buf, sems):
+def pieces(length, size, first=0):
+    edges = [0] + list(range(first or size, length, size)) + [length]
+    return [slice(a, b) for a, b in zip(edges[:-1], edges[1:])]
+
+
+def sends(buf, out, sems, ats):
+    return [pltpu.make_async_copy(buf.at[:, :, at], out.at[:, :, at], sems.at[i]) for i, at in enumerate(ats)]
+
+
+def spectrum_kernel(f_hbm, table_hbm, out_hbm, f_buf, table_buf, out_ref, sems, out_sems):
     freq = out_ref.shape[0]
     points, receivers, _ = f_buf.shape
-    ats = pieces(receivers, 256)
+    ats = pieces(receivers, 512, 256)
+    outs = sends(out_ref, out_hbm, out_sems, ats)
     copies = [pltpu.make_async_copy(f_hbm.at[:, at], f_buf.at[:, at], sems.at[i]) for i, at in enumerate(ats)]
     table_copy = pltpu.make_async_copy(table_hbm, table_buf, sems.at[len(ats)])
     table_copy.start()
@@ -84,6 +90,9 @@
         parts = [dot(table_buf[...], f_buf[p, at], NT) for p in range(points)]
         parts = [s.reshape(freq, s.shape[0] // freq, s.shape[1]) for s in parts]
         out_ref[:, :, at] = jnp.concatenate(parts, axis=1).astype(BF16)
+        outs[i].start()
+    for copy in outs:
+        copy.wait()
 
 
 def spectrum(f, table, freq):
@@ -92,12 +101,14 @@
     return pl.pallas_call(
         spectrum_kernel,
         in_specs=[ANY, ANY],
-        out_specs=VSPEC,
+        out_specs=ANY,
         out_shape=jax.ShapeDtypeStruct((freq, rows, receivers), BF16),
         scratch_shapes=[
             pltpu.VMEM(f.shape, BF16),
             pltpu.VMEM(table.shape, BF16),
-            pltpu.SemaphoreType.DMA((len(pieces(receivers, 256)) + 1,)),
+            pltpu.VMEM((freq, rows, receivers), BF16),
+            pltpu.SemaphoreType.DMA((len(pieces(receivers, 512, 256)) + 1,)),
+            pltpu.SemaphoreType.DMA((len(pieces(receivers, 512, 256)),)),
         ],
         compiler_params=PARAMS,
         cost_estimate=cost(2 * f.size * table.shape[0], 2 * (f.size + freq * rows * receivers)),
@@ -195,7 +206,7 @@
     )(vmem(v), vmem(onset), vmem(table))
 
 
-def adjoint_kernel(k_ref, u_ref, pairs_ref, order_ref, out_ref, o):
+def adjoint_kernel(k_ref, u_ref, pairs_ref, order_ref, out_ref, o, *rest):
     own, rows, receivers = o.shape
     half = rows // 2
     blocks, _, width = u_ref.shape
@@ -205,19 +216,33 @@
         l0 = dot(pairs_ref[...], jnp.concatenate(parts, axis=1), TN).astype(BF16)
         l1 = jnp.concatenate([l0[half:], -l0[:half]], axis=0)
         o[kk] = (dot(l0, k_ref[0, kk]) + dot(l1, k_ref[1, kk])).astype(BF16)
-    flat = o[...].reshape(own * rows, receivers)
-    out_ref[...] = dot(order_ref[...], flat, TN).astype(BF16).reshape(out_ref.shape)
-
-
-def adjoint(kernel, u, pairs, order, freq):
+    if not rest:
+        flat = o[...].reshape(own * rows, receivers)
+        out_ref[...] = dot(order_ref[...], flat, TN).astype(BF16).reshape(out_ref.shape)
+        return
+    out_buf, sems = rest
+    ats = pieces(receivers, 512)
+    outs = sends(out_buf, out_ref, sems, ats)
+    back = order_ref[...].T
+    for i, at in enumerate(ats):
+        piece = dot(back, o[:, :, at].reshape(own * rows, at.stop - at.start)).astype(BF16)
+        out_buf[:, :, at] = piece.reshape(out_buf.shape[:2] + piece.shape[1:])
+        outs[i].start()
+    for copy in outs:
+        copy.wait()
+
+
+def adjoint(kernel, u, pairs, order, freq, send):
     _, own, sources, receivers = kernel.shape
     rows = u.shape[1]
+    out = (freq, own * rows // freq, receivers)
+    sending = [pltpu.VMEM(out, BF16), pltpu.SemaphoreType.DMA((len(pieces(receivers, 512)),))]
     return pl.pallas_call(
         adjoint_kernel,
         in_specs=[VSPEC] * 4,
-        out_specs=VSPEC,
-        out_shape=jax.ShapeDtypeStruct((freq, own * rows // freq, receivers), BF16),
-        scratch_shapes=[pltpu.VMEM((own, rows, receivers), BF16)],
+        out_specs=ANY if send else VSPEC,
+        out_shape=jax.ShapeDtypeStruct(out, BF16),
+        scratch_shapes=[pltpu.VMEM((own, rows, receivers), BF16)] + (sending if send else []),
         compiler_params=PARAMS,
         cost_estimate=cost(2 * kernel.size * rows, 2 * own * rows * receivers),
         name="adjoint",
@@ -247,13 +272,15 @@
     return mine.reshape(freq * each, block).astype(BF16)
 
 
-def respectrum_kernel(block, q_ref, first_hbm, onset_ref, table_ref, across_ref, out_ref, first_ref, sem):
+def respectrum_kernel(block, q_ref, first_hbm, onset_ref, table_ref, across_ref, out_hbm, first_ref, out_ref, sem, out_sems):
     copy = pltpu.make_async_copy(first_hbm, first_ref, sem)
     copy.start()
     freq, rows, receivers = q_ref.shape
     samples, _ = across_ref.shape
     points = onset_ref.shape[0]
-    for i, at in enumerate(pieces(receivers, block)):
+    ats = pieces(receivers, block)
+    outs = sends(out_ref, out_hbm, out_sems, ats)
+    for i, at in enumerate(ats):
         wide = at.stop - at.start
         times = lax.broadcasted_iota(jnp.int32, (samples, wide), 0)
         parts = []
@@ -264,6 +291,9 @@
         if i == 0:
             copy.wait()
         out_ref[:, :, at] = (first_ref[:, :, at].astype(F32) + jnp.concatenate(parts, axis=1)).astype(BF16)
+        outs[i].start()
+    for copy in outs:
+        copy.wait()
 
 
 def respectrum(q, first, onset, table, across, block=512):
@@ -271,9 +301,14 @@
     return pl.pallas_call(
         functools.partial(respectrum_kernel, block),
         in_specs=[VSPEC, ANY, VSPEC, VSPEC, VSPEC],
-        out_specs=VSPEC,
+        out_specs=ANY,
         out_shape=jax.ShapeDtypeStruct(q.shape, BF16),
-        scratch_shapes=[pltpu.VMEM(q.shape, BF16), pltpu.SemaphoreType.DMA],
+        scratch_shapes=[
+            pltpu.VMEM(q.shape, BF16),
+            pltpu.VMEM(q.shape, BF16),
+            pltpu.SemaphoreType.DMA,
+            pltpu.SemaphoreType.DMA((len(pieces(receivers, block)),)),
+        ],
         compiler_params=PARAMS,
         cost_estimate=cost(4 * q.size * table.shape[1], 6 * q.size),
         name="respectrum",
@@ -327,7 +362,7 @@
         v = exchange(part.reshape(rec * freq, points * 2, width), ("rec", "freq")).reshape(rec, lines, width)
         h, *field = source_step(v, src_onsets, table, last, rec)
         u = exchange(h.reshape(rec * freq, points * 2, width), ("rec", "freq")).reshape(rec, lines, width)
-        q = adjoint(held, u, pairs, order, freq)
+        q = adjoint(held, u, pairs, order, freq, not last)
         if last:
             return update(exchange(q, "freq"), focusing_in, late, table), field[0]
         row, across = after(onset_rec, q)[:, None, :], lax.optimization_barrier(table).T

time: 274 us -> 272 us (level)
  no operation moved by 1% of the time
where the time goes in v3:
time: 272 us
  blocking collectives  125 us (46%)
  waiting for transfers between devices  91.4 us (34%)
  Pallas kernels  30.8 us (11%)
  starting transfers between devices  22.8 us (8%)
    all_to_all x5, blocking collectives, exchange(): return lax.all_to_all(x, axis, split_axis=0, concat_axis=0, tiled=True)  125 us
    all_to_all x3, waiting for transfers between devices, exchange(): return lax.all_to_all(x, axis, split_axis=0, concat_axis=0, tiled=True)  91.4 us
    all_to_all x3, starting transfers between devices, exchange(): return lax.all_to_all(x, axis, split_axis=0, concat_axis=0, tiled=True)  22.8 us
    pallas_call x2, Pallas kernels, product(): pl.pallas_call(product_kernel, in_specs=[ANY, VSPEC, VSPEC, VSPEC, ANY],...  8.52 us
  transfers between devices with their start and end apart: 3, of which 3 were waited for; matrix products, arithmetic and copies ran while one was open for 0% of the time, Pallas kernels for 0%

profile of v3, /device:TPU:1, one launch (start us, length us, event | category | flops | bytes accessed | tf_op | source)
XLA Modules:
  0.0 271.6 jit_solution(6905418262233947278)
XLA Ops:
  0.6 5.0 %spectrum.1.late_ref.first_hbm = bf16[32,16,1152]{2,1,0:T(8,128)(2,1)} custom-call(bf16[2,1152,1024]{2,1,0:T(8,128)(2,1)} %f_ref.1, bf16[256,1024]{1,0:T(8,128)(2,1)} %constant.16.clone.table_hbm.table_ref), custom_call_target="tpu_custom_call" | custom-call | flops 1207959552 | bytes 5898240 | tf_op jit(solution)/shard_map/spectrum/pallas_call | solution.py:101
  5.6 0.0 copy-start.4
  5.6 12.6 %all-to-all-start = ((bf16[32,16,1152]{2,1,0:T(8,128)(2,1)}), bf16[32,16,1152]{2,1,0:T(8,128)(2,1)S(1)}, u32[]{:S(2)}, u32[]{:S(2)}) async-start(bf16[32,16,1152]{2,1,0:T(8,128)(2,1)} %spectrum.1.late_ref.first_hbm), calls=%async_computation | async-start | bytes 2359296 | tf_op jit(solution)/shard_map/all_to_all | solution.py:343
  18.2 0.0 copy-done.4
  18.2 0.0 copy-start
  18.3 0.0 copy-start.2
  18.3 0.1 dynamic-slice_bitcast_fusion
  18.4 0.1 copy.13.late_ref.onset_ref
  18.5 0.0 copy-start.1
  18.5 30.6 %all-to-all-done.x_ref = bf16[32,16,1152]{2,1,0:T(8,128)(2,1)S(1)} async-done(((bf16[32,16,1152]{2,1,0:T(8,128)(2,1)}), bf16[32,16,1152]{2,1,0:T(8,128)(2,1)S(1)}, u32[]{:S(2)}, u32[]{:S(2)}) %all-to-all-start) | async-done | bytes 1179680 | tf_op jit(solution)/shard_map/all_to_all | solution.py:343
  49.1 0.0 copy-done
  49.1 0.0 copy-done.2
  49.1 4.3 %product.2 = (bf16[8,128,128]{2,1,0:T(8,128)(2,1)S(1)}, bf16[2,4,256,1152]{3,2,1,0:T(8,128)(2,1)S(1)}) custom-call(bf16[2,4,256,1152]{3,2,1,0:T(8,128)(2,1)} %k_hbm.3, bf16[32,16,1152]{2,1,0:T(8,128)(2,1)S(1)} %all-to-all-done.x_ref, bf16[512,512]{1,0:T(8,128)(2,1)S(1)} %copy-done, bf16[128,128]{1,0:T(8,128)(2,1)S(1)} %copy-done.2, ...), custom_call_target="tpu_custom_call" | custom-call | flops 603979776 | bytes 5898240 | tf_op jit(solution)/shard_map/product/pallas_call | solution.py:147
  53.4 24.3 %all_to_all.40 = bf16[256,4,128]{2,1,0:T(4,128)(2,1)S(1)} all-to-all(bf16[256,4,128]{2,1,0:T(4,128)(2,1)S(1)} %bitcast.19), channel_id=1, replica_groups=mesh['freq'=32,'rec'=8] {'rec','freq'}, dimensions={0} | all-to-all | bytes 524288 | tf_op jit(solution)/shard_map/all_to_all | solution.py:343
  77.6 0.0 copy-done.1
  77.6 1.5 source.2
  79.2 20.6 %all_to_all.41 = bf16[256,4,128]{2,1,0:T(4,128)(2,1)S(1)} all-to-all(bf16[256,4,128]{2,1,0:T(4,128)(2,1)S(1)} %bitcast.22), channel_id=1, replica_groups=mesh['freq'=32,'rec'=8] {'rec','freq'}, dimensions={0} | all-to-all | bytes 524288 | tf_op jit(solution)/shard_map/all_to_all | solution.py:343
  99.8 3.0 %adjoint.2.late_ref = bf16[32,16,1152]{2,1,0:T(8,128)(2,1)} custom-call(bf16[2,4,256,1152]{3,2,1,0:T(8,128)(2,1)S(1)} %get-tuple-element.8.k_ref, bf16[8,128,128]{2,1,0:T(8,128)(2,1)S(1)} %bitcast.16, bf16[128,128]{1,0:T(8,128)(2,1)S(1)} %copy-done.2, bf16[512,512]{1,0:T(8,128)(2,1)S(1)} %copy-done), custom_call_target="tpu_custom_call" | custom-call | flops 603979776 | bytes 1179648 | tf_op jit(solution)/shard_map/adjoint/pallas_call | solution.py:240
  102.8 0.0 copy-start.3
  102.8 4.1 %all-to-all-start.3 = ((bf16[32,16,1152]{2,1,0:T(8,128)(2,1)}), bf16[32,16,1152]{2,1,0:T(8,128)(2,1)S(1)}, u32[]{:S(2)}, u32[]{:S(2)}) async-start(bf16[32,16,1152]{2,1,0:T(8,128)(2,1)} %adjoint.2.late_ref), calls=%async_computation.3 | async-start | bytes 2359296 | tf_op jit(solution)/shard_map/all_to_all | solution.py:343
  106.9 0.2 copy.15.across_ref
  107.1 0.0 copy-done.3
  107.2 30.3 %all-to-all-done.3.q_ref = bf16[32,16,1152]{2,1,0:T(8,128)(2,1)S(1)} async-done(((bf16[32,16,1152]{2,1,0:T(8,128)(2,1)}), bf16[32,16,1152]{2,1,0:T(8,128)(2,1)S(1)}, u32[]{:S(2)}, u32[]{:S(2)}) %all-to-all-start.3) | async-done | bytes 1179680 | tf_op jit(solution)/shard_map/all_to_all | solution.py:343
  137.5 4.3 %respectrum.1.late_ref = bf16[32,16,1152]{2,1,0:T(8,128)(2,1)} custom-call(bf16[32,16,1152]{2,1,0:T(8,128)(2,1)S(1)} %all-to-all-done.3.q_ref, bf16[32,16,1152]{2,1,0:T(8,128)(2,1)} %spectrum.1.late_ref.first_hbm, s32[2,1,1152]{2,1,0:T(1,128)S(1)} %broadcast_in_dim.10.onset_ref, bf16[256,1024]{1,0:T(8,128)(2,1)S(1)} %copy-done.1, ...), custom_call_target="tpu_custom_call" | custom-call | flops 2415919104 | bytes 3538944 | tf_op jit(solution)/shard_map/respectrum/pallas_call | solution.py:301
  141.8 6.1 %all-to-all-start.4 = ((bf16[32,16,1152]{2,1,0:T(8,128)(2,1)}), bf16[32,16,1152]{2,1,0:T(8,128)(2,1)S(1)}, u32[]{:S(2)}, u32[]{:S(2)}) async-start(bf16[32,16,1152]{2,1,0:T(8,128)(2,1)} %respectrum.1.late_ref), calls=%async_computation.4 | async-start | bytes 2359296 | tf_op jit(solution)/shard_map/all_to_all | solution.py:343
  147.9 0.4 copy.16.late_ref.onset_ref
  148.3 30.4 %all-to-all-done.4.x_ref = bf16[32,16,1152]{2,1,0:T(8,128)(2,1)S(1)} async-done(((bf16[32,16,1152]{2,1,0:T(8,128)(2,1)}), bf16[32,16,1152]{2,1,0:T(8,128)(2,1)S(1)}, u32[]{:S(2)}, u32[]{:S(2)}) %all-to-all-start.4) | async-done | bytes 1179680 | tf_op jit(solution)/shard_map/all_to_all | solution.py:343
  178.8 4.3 %product.3 = (bf16[8,128,128]{2,1,0:T(8,128)(2,1)S(1)}, bf16[2,4,256,1152]{3,2,1,0:T(8,128)(2,1)S(1)}) custom-call(bf16[2,4,256,1152]{3,2,1,0:T(8,128)(2,1)} %k_hbm.3, bf16[32,16,1152]{2,1,0:T(8,128)(2,1)S(1)} %all-to-all-done.4.x_ref, bf16[512,512]{1,0:T(8,128)(2,1)S(1)} %copy-done, bf16[128,128]{1,0:T(8,128)(2,1)S(1)} %copy-done.2, ...), custom_call_target="tpu_custom_call" | custom-call | flops 603979776 | bytes 5898240 | tf_op jit(solution)/shard_map/product/pallas_call | solution.py:147
  183.0 22.8 %all_to_all.42 = bf16[256,4,128]{2,1,0:T(4,128)(2,1)S(1)} all-to-all(bf16[256,4,128]{2,1,0:T(4,128)(2,1)S(1)} %bitcast.20), channel_id=1, replica_groups=mesh['freq'=32,'rec'=8] {'rec','freq'}, dimensions={0} | all-to-all | bytes 524288 | tf_op jit(solution)/shard_map/all_to_all | solution.py:343
  205.9 0.0 slice-start
  205.9 2.0 source.3
  207.9 20.6 %all_to_all.43 = bf16[256,4,128]{2,1,0:T(4,128)(2,1)S(1)} all-to-all(bf16[256,4,128]{2,1,0:T(4,128)(2,1)S(1)} %bitcast.18), channel_id=1, replica_groups=mesh['freq'=32,'rec'=8] {'rec','freq'}, dimensions={0} | all-to-all | bytes 524288 | tf_op jit(solution)/shard_map/all_to_all | solution.py:343
  228.5 0.0 slice-start.1
  228.5 2.3 adjoint.3
  230.8 36.6 %all_to_all.44.q_ref = bf16[32,16,1152]{2,1,0:T(8,128)(2,1)S(1)} all-to-all(bf16[32,16,1152]{2,1,0:T(8,128)(2,1)S(1)} %adjoint.3), channel_id=1, replica_groups=mesh['freq'=32,'rec'=8] {'freq'}, dimensions={0} | all-to-all | bytes 2359296 | tf_op jit(solution)/shard_map/all_to_all | solution.py:343
  267.4 0.0 slice-done
  267.4 0.0 slice-done.1
  267.4 4.2 %update.1 = bf16[2,1152,1024]{2,1,0:T(8,128)(2,1)} custom-call(bf16[32,16,1152]{2,1,0:T(8,128)(2,1)S(1)} %all_to_all.44.q_ref, bf16[2,1152,1024]{2,1,0:T(8,128)(2,1)S(1)} %bitcast.13, s32[2,1152,1]{2,1,0:T(8,128)S(1)} %copy.16.late_ref.onset_ref, bf16[256,1024]{1,0:T(8,128)(2,1)S(1)} %copy-done.1), custom_call_target="tpu_custom_call" | custom-call | flops 1207959552 | bytes 10616832 | tf_op jit(solution)/shard_map/update/pallas_call | solution.py:330
  (5 shorter events, 0.0 us)
Async XLA Ops:
  5.6 12.6 %copy-start.4 = (s32[2,256]{1,0:T(2,128)S(1)}, s32[2,256]{1,0:T(2,128)}, u32[]{:S(2)}) copy-start(s32[2,256]{1,0:T(2,128)} %x_ref.3) | copy-start | bytes 6148
  5.6 43.4 %all-to-all-start = ((bf16[32,16,1152]{2,1,0:T(8,128)(2,1)}), bf16[32,16,1152]{2,1,0:T(8,128)(2,1)S(1)}, u32[]{:S(2)}, u32[]{:S(2)}) async-start(bf16[32,16,1152]{2,1,0:T(8,128)(2,1)} %spectrum.1.late_ref.first_hbm), calls=%async_computation | async-start | bytes 2359296 | tf_op jit(solution)/shard_map/all_to_all | solution.py:343
  18.2 30.8 %copy-start = (bf16[512,512]{1,0:T(8,128)(2,1)S(1)}, bf16[512,512]{1,0:T(8,128)(2,1)}, u32[]{:S(2)}) copy-start(bf16[512,512]{1,0:T(8,128)(2,1)} %constant.17.clone.order_ref) | copy-start | bytes 1572868
  18.3 30.8 %copy-start.2 = (bf16[128,128]{1,0:T(8,128)(2,1)S(1)}, bf16[128,128]{1,0:T(8,128)(2,1)}, u32[]{:S(2)}) copy-start(bf16[128,128]{1,0:T(8,128)(2,1)} %constant.18.clone.pairs_ref) | copy-start | bytes 98308
  18.5 59.2 %copy-start.1 = (bf16[256,1024]{1,0:T(8,128)(2,1)S(1)}, bf16[256,1024]{1,0:T(8,128)(2,1)}, u32[]{:S(2)}) copy-start(bf16[256,1024]{1,0:T(8,128)(2,1)} %constant.16.clone.table_hbm.table_ref) | copy-start | bytes 1572868
  102.8 4.3 %copy-start.3 = (s32[2,1152]{1,0:T(2,128)S(1)}, s32[2,1152]{1,0:T(2,128)}, u32[]{:S(2)}) copy-start(s32[2,1152]{1,0:T(2,128)} %x_ref.5) | copy-start | bytes 27652
  102.8 34.6 %all-to-all-start.3 = ((bf16[32,16,1152]{2,1,0:T(8,128)(2,1)}), bf16[32,16,1152]{2,1,0:T(8,128)(2,1)S(1)}, u32[]{:S(2)}, u32[]{:S(2)}) async-start(bf16[32,16,1152]{2,1,0:T(8,128)(2,1)} %adjoint.2.late_ref), calls=%async_computation.3 | async-start | bytes 2359296 | tf_op jit(solution)/shard_map/all_to_all | solution.py:343
  141.8 37.0 %all-to-all-start.4 = ((bf16[32,16,1152]{2,1,0:T(8,128)(2,1)}), bf16[32,16,1152]{2,1,0:T(8,128)(2,1)S(1)}, u32[]{:S(2)}, u32[]{:S(2)}) async-start(bf16[32,16,1152]{2,1,0:T(8,128)(2,1)} %respectrum.1.late_ref), calls=%async_computation.4 | async-start | bytes 2359296 | tf_op jit(solution)/shard_map/all_to_all | solution.py:343
  205.9 61.5 %slice-start = ((s8[4718592]{0:T(1024)(128)(4,1)}), s8[4194304]{0:T(1024)(128)(4,1)S(1)}, s32[]{:S(2)}) async-start(s8[4718592]{0:T(1024)(128)(4,1)} %bitcast.12), calls=%async_computation.8 | async-start | bytes 8388608
  228.5 38.9 %slice-start.1 = ((s8[4718592]{0:T(1024)(128)(4,1)}), s8[524288]{0:T(1024)(128)(4,1)S(1)}, s32[]{:S(2)}) async-start(s8[4718592]{0:T(1024)(128)(4,1)} %bitcast.12), calls=%async_computation.9 | async-start | bytes 1048576

commit v4 on v3

--- a/solution.py
+++ b/solution.py
@@ -318,10 +318,13 @@
 def update_kernel(q_ref, f_ref, onset_ref, table_ref, out_ref):
     points, block, samples = f_ref.shape
     at = pl.ds(pl.program_id(0) * block, block)
+    lanes = 128
     times = lax.broadcasted_iota(jnp.int32, (block, samples), 1)
     for p in range(points):
+        column = jnp.broadcast_to(onset_ref[p, :, at], (lanes, block)).T
+        onset = jnp.concatenate([column] * (samples // lanes), axis=1)
         q = dot(own_rows(q_ref[:, :, at], points, p, 2.0 / samples), table_ref[...], TN)
-        out_ref[p] = (f_ref[p].astype(F32) + jnp.where(times < onset_ref[p], q, 0.0)).astype(BF16)
+        out_ref[p] = (f_ref[p].astype(F32) + jnp.where(times < onset, q, 0.0)).astype(BF16)
 
 
 def update(q, f, onset, table, block=384):
@@ -330,13 +333,13 @@
     return pl.pallas_call(
         update_kernel,
         grid=(receivers // block,),
-        in_specs=[VSPEC, trace_block, pl.BlockSpec((points, block, 1), lambda i: (0, i, 0)), VSPEC],
+        in_specs=[VSPEC, trace_block, VSPEC, VSPEC],
         out_specs=trace_block,
         out_shape=jax.ShapeDtypeStruct(f.shape, BF16),
         compiler_params=PARAMS,
         cost_estimate=cost(2 * f.size * table.shape[0], 2 * (2 * f.size + q.size)),
         name="update",
-    )(vmem(q), f, onset, vmem(table))
+    )(vmem(q), f, vmem(onset), vmem(table))
 
 
 def exchange(x, axis):
@@ -364,10 +367,9 @@
         u = exchange(h.reshape(rec * freq, points * 2, width), ("rec", "freq")).reshape(rec, lines, width)
         q = adjoint(held, u, pairs, order, freq, not last)
         if last:
-            return update(exchange(q, "freq"), focusing_in, late, table), field[0]
+            return update(exchange(q, "freq"), focusing_in, row, table), field[0]
         row, across = after(onset_rec, q)[:, None, :], lax.optimization_barrier(table).T
         spec = respectrum(exchange(q, "freq"), start, row, table, across)
-        late = after(onset_rec, spec)[:, :, None]
 
 
 def solution(mesh):

time: 272 us -> 272 us (level)
  blocking collectives: 125 us -> 162 us
  waiting for transfers between devices: 91.4 us -> 60.9 us
  starting transfers between devices: 22.8 us -> 16.6 us
    all_to_all x5 -> x6, blocking collectives: 125 us -> 162 us  [exchange(): return lax.all_to_all(x, axis, split_axis=0, concat_axis=0, tiled=True)]
    all_to_all x3 -> x2, waiting for transfers between devices: 91.4 us -> 60.9 us  [exchange(): return lax.all_to_all(x, axis, split_axis=0, concat_axis=0, tiled=True)]
    all_to_all x3 -> x2, starting transfers between devices: 22.8 us -> 16.6 us  [exchange(): return lax.all_to_all(x, axis, split_axis=0, concat_axis=0, tiled=True)]
  transfers between devices with their start and end apart: 3 -> 2, of which waited for: 3 -> 2; matrix products, arithmetic and copies ran while one was open for 0% -> 0% of each run, Pallas kernels for 0% -> 0%
where the time goes in v4:
time: 272 us; the launch traced here: 271 us
  blocking collectives  162 us (60%)
  waiting for transfers between devices  60.9 us (22%)
  Pallas kernels  30.4 us (11%)
  starting transfers between devices  16.6 us (6%)
    all_to_all x6, blocking collectives, exchange(): return lax.all_to_all(x, axis, split_axis=0, concat_axis=0, tiled=True)  162 us
    all_to_all x2, waiting for transfers between devices, exchange(): return lax.all_to_all(x, axis, split_axis=0, concat_axis=0, tiled=True)  60.9 us
    all_to_all x2, starting transfers between devices, exchange(): return lax.all_to_all(x, axis, split_axis=0, concat_axis=0, tiled=True)  16.6 us
    pallas_call x2, Pallas kernels, product(): pl.pallas_call(product_kernel, in_specs=[ANY, VSPEC, VSPEC, VSPEC, ANY],...  8.52 us
  transfers between devices with their start and end apart: 2, of which 2 were waited for; matrix products, arithmetic and copies ran while one was open for 0% of the time, Pallas kernels for 0%

profile of v4, /device:TPU:1, one launch (start us, length us, event | category | flops | bytes accessed | tf_op | source)
XLA Modules:
  0.0 271.4 jit_solution(15726129193231067232)
XLA Ops:
  0.6 5.0 %spectrum.1.late_ref.first_hbm = bf16[32,16,1152]{2,1,0:T(8,128)(2,1)} custom-call(bf16[2,1152,1024]{2,1,0:T(8,128)(2,1)} %f_ref.1, bf16[256,1024]{1,0:T(8,128)(2,1)} %constant.16.clone.table_hbm.table_ref), custom_call_target="tpu_custom_call" | custom-call | flops 1207959552 | bytes 5898240 | tf_op jit(solution)/shard_map/spectrum/pallas_call | solution.py:101
  5.6 0.0 copy-start.4
  5.6 12.6 %all-to-all-start = ((bf16[32,16,1152]{2,1,0:T(8,128)(2,1)}), bf16[32,16,1152]{2,1,0:T(8,128)(2,1)S(1)}, u32[]{:S(2)}, u32[]{:S(2)}) async-start(bf16[32,16,1152]{2,1,0:T(8,128)(2,1)} %spectrum.1.late_ref.first_hbm), calls=%async_computation | async-start | bytes 2359296 | tf_op jit(solution)/shard_map/all_to_all | solution.py:346
  18.2 0.0 copy-done.4
  18.2 0.0 copy-start
  18.3 0.0 copy-start.2
  18.3 0.1 dynamic-slice_bitcast_fusion
  18.4 0.1 copy.9.late_ref.onset_ref
  18.5 0.0 copy-start.1
  18.5 30.6 %all-to-all-done.x_ref = bf16[32,16,1152]{2,1,0:T(8,128)(2,1)S(1)} async-done(((bf16[32,16,1152]{2,1,0:T(8,128)(2,1)}), bf16[32,16,1152]{2,1,0:T(8,128)(2,1)S(1)}, u32[]{:S(2)}, u32[]{:S(2)}) %all-to-all-start) | async-done | bytes 1179680 | tf_op jit(solution)/shard_map/all_to_all | solution.py:346
  49.1 0.0 copy-done
  49.1 0.0 copy-done.2
  49.1 4.3 %product.2 = (bf16[8,128,128]{2,1,0:T(8,128)(2,1)S(1)}, bf16[2,4,256,1152]{3,2,1,0:T(8,128)(2,1)S(1)}) custom-call(bf16[2,4,256,1152]{3,2,1,0:T(8,128)(2,1)} %k_hbm.3, bf16[32,16,1152]{2,1,0:T(8,128)(2,1)S(1)} %all-to-all-done.x_ref, bf16[512,512]{1,0:T(8,128)(2,1)S(1)} %copy-done, bf16[128,128]{1,0:T(8,128)(2,1)S(1)} %copy-done.2, ...), custom_call_target="tpu_custom_call" | custom-call | flops 603979776 | bytes 5898240 | tf_op jit(solution)/shard_map/product/pallas_call | solution.py:147
  53.4 24.3 %all_to_all.40 = bf16[256,4,128]{2,1,0:T(4,128)(2,1)S(1)} all-to-all(bf16[256,4,128]{2,1,0:T(4,128)(2,1)S(1)} %bitcast.18), channel_id=1, replica_groups=mesh['freq'=32,'rec'=8] {'rec','freq'}, dimensions={0} | all-to-all | bytes 524288 | tf_op jit(solution)/shard_map/all_to_all | solution.py:346
  77.6 0.0 copy-done.1
  77.6 1.5 source.2
  79.2 20.6 %all_to_all.41 = bf16[256,4,128]{2,1,0:T(4,128)(2,1)S(1)} all-to-all(bf16[256,4,128]{2,1,0:T(4,128)(2,1)S(1)} %bitcast.21), channel_id=1, replica_groups=mesh['freq'=32,'rec'=8] {'rec','freq'}, dimensions={0} | all-to-all | bytes 524288 | tf_op jit(solution)/shard_map/all_to_all | solution.py:346
  99.8 3.0 %adjoint.2.late_ref = bf16[32,16,1152]{2,1,0:T(8,128)(2,1)} custom-call(bf16[2,4,256,1152]{3,2,1,0:T(8,128)(2,1)S(1)} %get-tuple-element.8.k_ref, bf16[8,128,128]{2,1,0:T(8,128)(2,1)S(1)} %bitcast.15, bf16[128,128]{1,0:T(8,128)(2,1)S(1)} %copy-done.2, bf16[512,512]{1,0:T(8,128)(2,1)S(1)} %copy-done), custom_call_target="tpu_custom_call" | custom-call | flops 603979776 | bytes 1179648 | tf_op jit(solution)/shard_map/adjoint/pallas_call | solution.py:240
  102.8 0.0 copy-start.3
  102.8 4.1 %all-to-all-start.3 = ((bf16[32,16,1152]{2,1,0:T(8,128)(2,1)}), bf16[32,16,1152]{2,1,0:T(8,128)(2,1)S(1)}, u32[]{:S(2)}, u32[]{:S(2)}) async-start(bf16[32,16,1152]{2,1,0:T(8,128)(2,1)} %adjoint.2.late_ref), calls=%async_computation.3 | async-start | bytes 2359296 | tf_op jit(solution)/shard_map/all_to_all | solution.py:346
  106.9 0.2 copy.11.across_ref
  107.1 0.0 copy-done.3
  107.1 30.3 %all-to-all-done.3.q_ref = bf16[32,16,1152]{2,1,0:T(8,128)(2,1)S(1)} async-done(((bf16[32,16,1152]{2,1,0:T(8,128)(2,1)}), bf16[32,16,1152]{2,1,0:T(8,128)(2,1)S(1)}, u32[]{:S(2)}, u32[]{:S(2)}) %all-to-all-start.3) | async-done | bytes 1179680 | tf_op jit(solution)/shard_map/all_to_all | solution.py:346
  137.5 3.9 %respectrum.1 = bf16[32,16,1152]{2,1,0:T(8,128)(2,1)S(1)} custom-call(bf16[32,16,1152]{2,1,0:T(8,128)(2,1)S(1)} %all-to-all-done.3.q_ref, bf16[32,16,1152]{2,1,0:T(8,128)(2,1)} %spectrum.1.late_ref.first_hbm, s32[2,1,1152]{2,1,0:T(1,128)S(1)} %broadcast_in_dim.7.onset_ref, bf16[256,1024]{1,0:T(8,128)(2,1)S(1)} %copy-done.1, ...), custom_call_target="tpu_custom_call" | custom-call | flops 2415919104 | bytes 3538944 | tf_op jit(solution)/shard_map/respectrum/pallas_call | solution.py:301
  141.3 38.7 %all_to_all.42.x_ref = bf16[32,16,1152]{2,1,0:T(8,128)(2,1)S(1)} all-to-all(bf16[32,16,1152]{2,1,0:T(8,128)(2,1)S(1)} %respectrum.1), channel_id=1, replica_groups=mesh['freq'=32,'rec'=8] {'freq'}, dimensions={0} | all-to-all | bytes 2359296 | tf_op jit(solution)/shard_map/all_to_all | solution.py:346
  180.0 4.3 %product.3 = (bf16[8,128,128]{2,1,0:T(8,128)(2,1)S(1)}, bf16[2,4,256,1152]{3,2,1,0:T(8,128)(2,1)S(1)}) custom-call(bf16[2,4,256,1152]{3,2,1,0:T(8,128)(2,1)} %k_hbm.3, bf16[32,16,1152]{2,1,0:T(8,128)(2,1)S(1)} %all_to_all.42.x_ref, bf16[512,512]{1,0:T(8,128)(2,1)S(1)} %copy-done, bf16[128,128]{1,0:T(8,128)(2,1)S(1)} %copy-done.2, ...), custom_call_target="tpu_custom_call" | custom-call | flops 603979776 | bytes 5898240 | tf_op jit(solution)/shard_map/product/pallas_call | solution.py:147
  184.3 21.4 %all_to_all.43 = bf16[256,4,128]{2,1,0:T(4,128)(2,1)S(1)} all-to-all(bf16[256,4,128]{2,1,0:T(4,128)(2,1)S(1)} %bitcast.19), channel_id=1, replica_groups=mesh['freq'=32,'rec'=8] {'rec','freq'}, dimensions={0} | all-to-all | bytes 524288 | tf_op jit(solution)/shard_map/all_to_all | solution.py:346
  205.7 0.0 slice-start
  205.7 2.0 source.3
  207.7 20.6 %all_to_all.44 = bf16[256,4,128]{2,1,0:T(4,128)(2,1)S(1)} all-to-all(bf16[256,4,128]{2,1,0:T(4,128)(2,1)S(1)} %bitcast.17), channel_id=1, replica_groups=mesh['freq'=32,'rec'=8] {'rec','freq'}, dimensions={0} | all-to-all | bytes 524288 | tf_op jit(solution)/shard_map/all_to_all | solution.py:346
  228.3 0.0 slice-start.1
  228.3 2.3 adjoint.3
  230.6 36.6 %all_to_all.45.q_ref = bf16[32,16,1152]{2,1,0:T(8,128)(2,1)S(1)} all-to-all(bf16[32,16,1152]{2,1,0:T(8,128)(2,1)S(1)} %adjoint.3), channel_id=1, replica_groups=mesh['freq'=32,'rec'=8] {'freq'}, dimensions={0} | all-to-all | bytes 2359296 | tf_op jit(solution)/shard_map/all_to_all | solution.py:346
  267.2 0.0 slice-done
  267.2 0.0 slice-done.1
  267.2 4.1 %update.1 = bf16[2,1152,1024]{2,1,0:T(8,128)(2,1)} custom-call(bf16[32,16,1152]{2,1,0:T(8,128)(2,1)S(1)} %all_to_all.45.q_ref, bf16[2,1152,1024]{2,1,0:T(8,128)(2,1)S(1)} %bitcast.12, s32[2,1,1152]{2,1,0:T(1,128)S(1)} %broadcast_in_dim.7.onset_ref, bf16[256,1024]{1,0:T(8,128)(2,1)S(1)} %copy-done.1), custom_call_target="tpu_custom_call" | custom-call | flops 1207959552 | bytes 10616832 | tf_op jit(solution)/shard_map/update/pallas_call | solution.py:333
  (4 shorter events, 0.0 us)
Async XLA Ops:
  5.6 12.6 %copy-start.4 = (s32[2,256]{1,0:T(2,128)S(1)}, s32[2,256]{1,0:T(2,128)}, u32[]{:S(2)}) copy-start(s32[2,256]{1,0:T(2,128)} %x_ref.2) | copy-start | bytes 6148
  5.6 43.4 %all-to-all-start = ((bf16[32,16,1152]{2,1,0:T(8,128)(2,1)}), bf16[32,16,1152]{2,1,0:T(8,128)(2,1)S(1)}, u32[]{:S(2)}, u32[]{:S(2)}) async-start(bf16[32,16,1152]{2,1,0:T(8,128)(2,1)} %spectrum.1.late_ref.first_hbm), calls=%async_computation | async-start | bytes 2359296 | tf_op jit(solution)/shard_map/all_to_all | solution.py:346
  18.2 30.8 %copy-start = (bf16[512,512]{1,0:T(8,128)(2,1)S(1)}, bf16[512,512]{1,0:T(8,128)(2,1)}, u32[]{:S(2)}) copy-start(bf16[512,512]{1,0:T(8,128)(2,1)} %constant.17.clone.order_ref) | copy-start | bytes 1572868
  18.3 30.8 %copy-start.2 = (bf16[128,128]{1,0:T(8,128)(2,1)S(1)}, bf16[128,128]{1,0:T(8,128)(2,1)}, u32[]{:S(2)}) copy-start(bf16[128,128]{1,0:T(8,128)(2,1)} %constant.18.clone.pairs_ref) | copy-start | bytes 98308
  18.5 59.2 %copy-start.1 = (bf16[256,1024]{1,0:T(8,128)(2,1)S(1)}, bf16[256,1024]{1,0:T(8,128)(2,1)}, u32[]{:S(2)}) copy-start(bf16[256,1024]{1,0:T(8,128)(2,1)} %constant.16.clone.table_hbm.table_ref) | copy-start | bytes 1572868
  102.8 4.3 %copy-start.3 = (s32[2,1152]{1,0:T(2,128)S(1)}, s32[2,1152]{1,0:T(2,128)}, u32[]{:S(2)}) copy-start(s32[2,1152]{1,0:T(2,128)} %x_ref.3) | copy-start | bytes 27652
  102.8 34.6 %all-to-all-start.3 = ((bf16[32,16,1152]{2,1,0:T(8,128)(2,1)}), bf16[32,16,1152]{2,1,0:T(8,128)(2,1)S(1)}, u32[]{:S(2)}, u32[]{:S(2)}) async-start(bf16[32,16,1152]{2,1,0:T(8,128)(2,1)} %adjoint.2.late_ref), calls=%async_computation.3 | async-start | bytes 2359296 | tf_op jit(solution)/shard_map/all_to_all | solution.py:346
  205.7 61.5 %slice-start = ((s8[4718592]{0:T(1024)(128)(4,1)}), s8[4194304]{0:T(1024)(128)(4,1)S(1)}, s32[]{:S(2)}) async-start(s8[4718592]{0:T(1024)(128)(4,1)} %bitcast.11), calls=%async_computation.8 | async-start | bytes 8388608
  228.3 38.9 %slice-start.1 = ((s8[4718592]{0:T(1024)(128)(4,1)}), s8[524288]{0:T(1024)(128)(4,1)S(1)}, s32[]{:S(2)}) async-start(s8[4718592]{0:T(1024)(128)(4,1)} %bitcast.11), calls=%async_computation.9 | async-start | bytes 1048576
